TPU v7x, 256 devices: a whole 4x4x8 slice. The times are simulated.
256 devices in a mesh: station: 8 (over x, z_hi), tm: 32 (over y, z_lo, core).
Axes of the slice: x: 4, y: 4, z: 8 (z_hi: 2, z_lo: 4; z = z_hi * 4 + z_lo), core: 2. Of those that a mesh axis runs over, the one named last changes fastest.
Arguments:
- features: bfloat16 [4194304, 256], P(('station', 'tm')), may hold values from -8 to 8
- targets: bfloat16 [4194304], P(('station', 'tm')), may hold values from -6 to 6
- station_ids: int32 [4194304], P(('station', 'tm')), may hold values from 0 to 127
- lead_heads: int32 [4194304], P(('station', 'tm')), may hold values from 0 to 15, as said below
- station_weight: float32 [8, 128], P('station'), may hold values from 0.2 to 5
Outputs:
- leverage: float32 [4194304], P(('station', 'tm'))
- zscores: float32 [16, 256], replicated
- inverse_factor: float32 [16, 256, 256], P(None, 'tm')
Inputs may be any that keep to these rules, and one draw needn't show every extreme that they name: lead_heads is constant over each aligned block of 1024 rows.
All inputs are finite; a program needn't handle non-finite values.
Results may differ from a plain program's by a relative error of at most 0.008.
Values sent between devices are 32-bit elements; how exact they have to be, the bound alone decides.
No kernel may reach another device: no remote copies, remote signals or barrier semaphores. Data moves between devices by JAX's collectives and lax.ppermute only.
A program may use at most 128 MiB of HBM per device.

v0:
```python
import math

import jax
import jax.numpy as jnp
from jax import lax
from jax.sharding import PartitionSpec as P

HEADS = 16
BLK = 1024


def factor_heads(gram_sum, moment):
    feat_width = gram_sum.shape[-1]
    identity = jnp.eye(feat_width, dtype=jnp.float32)
    lower_factor = jnp.linalg.cholesky(gram_sum + identity)
    inverse = lax.linalg.triangular_solve(
        lower_factor, jnp.broadcast_to(identity, gram_sum.shape), left_side=True, lower=True
    )
    inner_term = jnp.einsum("hkj,hj->hk", inverse, moment, precision=lax.Precision.HIGHEST)
    coefficient = jnp.einsum("hkj,hk->hj", inverse, inner_term, precision=lax.Precision.HIGHEST)
    spreads = jnp.sqrt(jnp.sum(inverse * inverse, axis=1))
    return (inverse, coefficient / spreads)


def local(features, targets, station_ids, lead_heads, station_weight):
    row_count, feat_width = features.shape
    station_count = station_weight.shape[1]
    block_count = row_count // BLK
    total_rows = row_count * lax.axis_size("station") * lax.axis_size("tm")
    station_pick = (
        station_ids[:, None] == jnp.arange(station_count, dtype=jnp.int32)[None, :]
    ).astype(jnp.float32)
    row_weight = jnp.dot(station_pick, station_weight[0], precision=lax.Precision.HIGHEST)
    weighted = (row_weight[:, None] * features).astype(jnp.bfloat16)
    feat_blocks = features.reshape(block_count, BLK, feat_width)
    weight_blocks = weighted.reshape(block_count, BLK, feat_width)
    target_blocks = targets.reshape(block_count, BLK)
    block_heads = lead_heads.reshape(block_count, BLK)[:, 0]
    block_pick = (block_heads[:, None] == jnp.arange(HEADS, dtype=jnp.int32)[None, :]).astype(
        jnp.float32
    )
    block_gram = jnp.einsum(
        "bri,brj->bij", weight_blocks, feat_blocks, preferred_element_type=jnp.float32
    )
    block_moment = jnp.einsum(
        "bri,br->bi", weight_blocks, target_blocks, preferred_element_type=jnp.float32
    )
    gram_sum = jnp.einsum("bh,bij->hij", block_pick, block_gram, precision=lax.Precision.HIGHEST)
    moment = jnp.einsum("bh,bi->hi", block_pick, block_moment, precision=lax.Precision.HIGHEST)
    gram_payload = gram_sum
    gram_payload, moment = lax.psum((gram_payload, moment), ("station", "tm"))
    inverse, zscores = factor_heads(gram_payload, moment)
    inverse_low = inverse.astype(jnp.bfloat16)
    picked = jnp.einsum(
        "bh,hkj->bkj",
        block_pick.astype(jnp.bfloat16),
        inverse_low,
        preferred_element_type=jnp.float32,
    ).astype(jnp.bfloat16)
    projected = jnp.einsum("bri,bki->brk", feat_blocks, picked, preferred_element_type=jnp.float32)
    sum_squares = jnp.sum(projected * projected, axis=2).reshape(row_count)
    leverage = row_weight * sum_squares * (total_rows / (HEADS * feat_width))
    piece_rows = feat_width // lax.axis_size("tm")
    own_piece = lax.dynamic_slice_in_dim(inverse, lax.axis_index("tm") * piece_rows, piece_rows, 1)
    inverse_factor = own_piece * math.sqrt(total_rows / HEADS)
    return (leverage, zscores, inverse_factor)


def solution(mesh):
    return jax.shard_map(
        local,
        mesh=mesh,
        in_specs=(
            P(("station", "tm"), None),
            P(("station", "tm")),
            P(("station", "tm")),
            P(("station", "tm")),
            P("station", None),
        ),
        out_specs=(P(("station", "tm")), P(), P(None, "tm", None)),
        check_vma=False,
    )
```

profile of v0, /device:TPU:1, one launch (start us, length us, event | category | flops | bytes accessed | tf_op | source)
XLA Modules:
  0.0 1233.9 jit_solution(11257697658252438608)
XLA Ops:
  7.2 0.9 reshape.53
  8.1 0.1 slice_reduce_fusion
  8.2 6.5 fusion
  14.7 7.9 multiply_convert_fusion
  22.6 8.2 fusion.44
  30.9 5.2 fusion.2
  36.1 5.2 copy.43
  41.4 0.7 copy-done.5
  42.2 0.1 copy.50
  42.4 4.6 fusion.45
  46.9 0.3 fusion.27
  47.2 82.0 %psum.15 = f32[16,256]{1,0:T(8,128)} all-reduce(f32[16,256]{1,0:T(8,128)S(1)} %fusion.27), channel_id=1, replica_groups=mesh['station'=8,'tm'=32] {'station','tm'}, use_global_device_ids=true, to_apply=%region_6.7 | all-reduce | flops 4096 | bytes 32768 | tf_op jit(solution)/shard_map/psum | solution.py:51
  129.2 0.6 iota_compare_fusion.5
  129.9 184.3 %all-reduce.3.cloned.1.call-done = f32[16,256,256]{1,2,0:T(8,128)} async-done(((f32[16,256,256]{1,2,0:T(8,128)}), f32[16,256,256]{1,2,0:T(8,128)}) %all-reduce.3.cloned.1.call-update) | async-done | bytes 4194320 | tf_op jit(solution)/shard_map/psum | solution.py:51
  314.2 4.6 broadcast_add_fusion
  318.7 5.3 copy.44
  324.1 4.0 fusion.1
  328.1 1.9 copy-done.2
  330.1 187.5 %custom-call.16 = f32[16,128,128]{2,1,0:T(8,128)S(1)} custom-call(f32[16,128,128]{2,1,0:T(8,128)S(1)} %cholesky.122), custom_call_target="Cholesky" | custom-call | tf_op jit(solution)/shard_map/jit(cholesky)/cholesky | solution.py:15
  517.7 0.1 select_bitcast_fusion
  517.8 157.2 %custom-call.17 = f32[16,1,128,128]{2,3,1,0:T(8,128)S(1)} custom-call(f32[16,1,128,128]{3,2,1,0:T(8,128)S(1)} %select_bitcast_fusion), custom_call_target="InvertDiagBlocksLowerTriangular" | custom-call | tf_op jit(solution)/shard_map/jit(cholesky)/cholesky | solution.py:15
  675.0 2.6 cholesky.117
  677.6 1.1 copy-done.3
  678.7 2.3 constant_dynamic-update-slice_fusion.1
  681.0 2.3 convolution_subtract_fusion
  683.3 187.8 %custom-call.18 = f32[16,128,128]{2,1,0:T(8,128)S(1)} custom-call(f32[16,128,128]{2,1,0:T(8,128)S(1)} %convolution_subtract_fusion), custom_call_target="Cholesky" | custom-call | tf_op jit(solution)/shard_map/jit(cholesky)/cholesky | solution.py:15
  871.0 2.0 select_reduce_fusion
  873.1 0.1 compare_reduce_fusion
  873.2 4.8 select_select_fusion
  878.0 9.3 while.1
  878.1 0.6 fusion.55
  878.6 4.2 bitcast_dynamic-update-slice_fusion.2
  882.9 0.6 fusion.55
  883.5 3.9 bitcast_dynamic-update-slice_fusion.2
  887.4 315.4 %custom-call.19 = f32[16,2,128,128]{2,3,1,0:T(8,128)S(1)} custom-call(f32[16,2,128,128]{3,2,1,0:T(8,128)} %bitcast.75), custom_call_target="InvertDiagBlocksLowerTriangular" | custom-call | tf_op jit(solution)/shard_map/triangular_solve | solution.py:16
  1202.7 1.9 fusion.18
  1204.6 3.2 fusion.16
  1207.8 2.1 fusion.8
  1209.9 0.3 multiply_reduce_fusion.1
  1210.2 0.3 fusion.12
  1210.5 0.4 copy-done.4
  1211.0 3.6 fusion.11
  1214.6 2.3 fusion.10
  1216.8 0.7 fusion.26
  1217.5 1.6 fusion.13
  1219.2 6.1 multiply_reduce_fusion
  1225.3 0.6 multiply_multiply_fusion
  1225.9 0.6 bitcast_multiply_fusion
  (25 shorter events, 0.5 us)
Async XLA Ops:
  7.2 1.0 copy-start
  7.2 307.0 %all-reduce.3.cloned.1.call-start = ((), (), s32[]{:S(2)}) async-start(), calls=%async_computation | async-start | bytes 8388608 | tf_op jit(solution)/shard_map/psum | solution.py:51
  41.3 0.8 copy-start.5
  328.1 1.9 copy-start.2
  675.0 3.7 copy-start.3
  1210.2 0.7 copy-start.4
  1219.2 7.4 copy-start.1
Sparse Core Ops, SparseCore 0:
  41.5 272.6 all-reduce.2
where the time goes:
time: 1240 us; the launch traced here: 1230 us
  other arithmetic  875 us (71%)
  waiting for transfers between devices  184 us (15%)
  blocking collectives  82 us (7%)
  matrix products  50.1 us (4%)
  local copies, waits for them, and re-layouts  28 us (2%)
  between operations  14.8 us (1%)
    another operation x9, other arithmetic, factor_heads(): lower_factor = jnp.linalg.cholesky(gram_sum + identity)  535 us
    another operation x4, other arithmetic, factor_heads(): lax.linalg.triangular_solve(lower_factor, jnp.broadcast_to(identity, gram...  320 us
    psum x1, waiting for transfers between devices, local(): gram_payload, moment = lax.psum((gram_payload, moment), ('station', 'tm'))  184 us
    psum x1, blocking collectives, local(): gram_payload, moment = lax.psum((gram_payload, moment), ('station', 'tm'))  82 us
  transfers between devices with their start and end apart: 1, of which 1 were waited for; matrix products, arithmetic and copies ran while one was open for 0% of the time, Pallas kernels for 0%

commit v1 on v0

v1 whole, which is shorter than its diff:
```python
import functools
import math

import jax
import jax.numpy as jnp
from jax import lax
from jax.experimental import pallas as pl
from jax.experimental.pallas import tpu as pltpu
from jax.sharding import Mesh, PartitionSpec as P

HEADS = 16
BLK = 1024
HALF = 128
PACKED = HALF + 8
EXACT = lax.Precision.HIGHEST
PLANE = ("x", "y")
COLUMN = ("zh", "zl")
COLUMN_SIZE = 8


def dot_nn(a, b):
    return lax.dot_general(
        a, b, (((1,), (0,)), ((), ())), precision=EXACT, preferred_element_type=jnp.float32
    )


def dot_nt(a, b):
    return lax.dot_general(
        a, b, (((1,), (1,)), ((), ())), precision=EXACT, preferred_element_type=jnp.float32
    )


def square_iotas():
    row_at = lax.broadcasted_iota(jnp.int32, (HALF, HALF), 0)
    col_at = lax.broadcasted_iota(jnp.int32, (HALF, HALF), 1)
    return row_at, col_at


def row_weights(table, ids):
    return jnp.take_along_axis(jnp.broadcast_to(table, ids.shape), ids, axis=1)


def gram_kernel(
    head_ref, core_ref, table_ref, id_ref, target_ref, feat_ref,
    keep_ref, send_ref, total_ref, moment_ref, pair_ref,
):
    step = pl.program_id(0)
    heads = total_ref.shape[0]

    @pl.when(step == 0)
    def _():
        total_ref[...] = jnp.zeros_like(total_ref)
        moment_ref[...] = jnp.zeros_like(moment_ref)

    weight = row_weights(table_ref[...], id_ref[...])
    target = target_ref[...]
    head = head_ref[step]
    flipped = feat_ref[...].T
    pieces = []
    for s in range(BLK // HALF):
        piece = flipped[:, s * HALF : (s + 1) * HALF].astype(jnp.float32) * weight[s : s + 1, :]
        pieces.append(piece.astype(jnp.bfloat16))
    weighted = jnp.concatenate(pieces, axis=1)
    total_ref[head] += jnp.dot(weighted, feat_ref[...], preferred_element_type=jnp.float32)
    target_row = jnp.concatenate([target[s : s + 1, :] for s in range(BLK // HALF)], axis=1)
    target_row = jnp.broadcast_to(target_row, (8, BLK)).astype(jnp.bfloat16)
    moment_ref[head] += lax.dot_general(
        target_row, weighted, (((1,), (1,)), ((), ())), preferred_element_type=jnp.float32
    )

    @pl.when(step == pl.num_programs(0) - 1)
    def _():
        core = core_ref[0]
        row_at, col_at = square_iotas()
        pair_ref[1, HALF:] = jnp.zeros((8, HALF), jnp.float32)
        for h in range(heads):
            second = total_ref[h, HALF:, HALF:]
            diag = jnp.sum(jnp.where(row_at == col_at, second, 0.0), axis=0, keepdims=True)
            moment = moment_ref[h, 0:1]
            pair_ref[0, :HALF] = total_ref[h, HALF:, :HALF]
            pair_ref[0, HALF:] = jnp.concatenate(
                [diag, moment[:, :HALF], moment[:, HALF:], jnp.zeros((5, HALF), jnp.float32)],
                axis=0,
            )
            pair_ref[1, :HALF] = jnp.where(col_at <= row_at, total_ref[h, :HALF, :HALF], second)
            keep_ref[h] = pair_ref[core]
            send_ref[h] = pair_ref[1 - core]


def gram_of(block_heads, core, table, ids, targets, features):
    rows, width = features.shape
    blocks = rows // BLK
    half = jax.ShapeDtypeStruct((HEADS, PACKED, HALF), jnp.float32)
    half_spec = pl.BlockSpec((HEADS, PACKED, HALF), lambda b, h, c: (0, 0, 0))
    return pl.pallas_call(
        gram_kernel,
        out_shape=(half, half),
        grid_spec=pltpu.PrefetchScalarGridSpec(
            num_scalar_prefetch=2,
            grid=(blocks,),
            in_specs=[
                pl.BlockSpec((1, HALF), lambda b, h, c: (0, 0)),
                pl.BlockSpec((BLK // HALF, HALF), lambda b, h, c: (b, 0)),
                pl.BlockSpec((BLK // HALF, HALF), lambda b, h, c: (b, 0)),
                pl.BlockSpec((BLK, width), lambda b, h, c: (b, 0)),
            ],
            out_specs=(half_spec, half_spec),
            scratch_shapes=[
                pltpu.VMEM((HEADS, width, width), jnp.float32),
                pltpu.VMEM((HEADS, 8, width), jnp.float32),
                pltpu.VMEM((2, PACKED, HALF), jnp.float32),
            ],
        ),
        cost_estimate=pl.CostEstimate(
            flops=2 * rows * width * width, bytes_accessed=2 * rows * width, transcendentals=0
        ),
        name="gram",
    )(block_heads, core, table, ids, targets, features)


def plane_sum_kernel(part_ref, out_ref):
    total = part_ref[0]
    for p in range(1, part_ref.shape[0]):
        total = total + part_ref[p]
    rows = HALF // COLUMN_SIZE
    for d in range(COLUMN_SIZE):
        out_ref[d, :rows] = total[d * rows : (d + 1) * rows]
        out_ref[d, rows:] = total[HALF:]


def column_sum_kernel(part_ref, out_ref, extra_ref):
    total = part_ref[0]
    for p in range(1, part_ref.shape[0]):
        total = total + part_ref[p]
    rows = HALF // COLUMN_SIZE
    for d in range(COLUMN_SIZE):
        out_ref[d] = total[:rows]
    extra_ref[...] = total[rows:]


def whole_call(kernel, out_shape, name, *args):
    vmem = pl.BlockSpec(memory_space=pltpu.VMEM)
    outs = jax.tree.map(lambda _: vmem, out_shape)
    return pl.pallas_call(
        kernel, out_shape=out_shape, in_specs=[vmem] * len(args), out_specs=outs, name=name
    )(*args)


def invert_factor(sym):
    row_at, col_at = square_iotas()
    on_diag = row_at == col_at
    diag_only = jnp.where(on_diag, sym, 0.0)
    scale_row = lax.rsqrt(jnp.sum(diag_only, axis=0, keepdims=True))
    scale_col = lax.rsqrt(jnp.sum(diag_only, axis=1, keepdims=True))
    work = sym * scale_row * scale_col
    tiles = [work[8 * t : 8 * t + 8, :] for t in range(HALF // 8)]
    lane = lax.broadcasted_iota(jnp.int32, (1, HALF), 1)
    sub = lax.broadcasted_iota(jnp.int32, (8, 1), 0)
    for k in range(HALF):
        t0, s0 = divmod(k, 8)
        row = tiles[t0][s0 : s0 + 1, :]
        recip = 1.0 / row[:, k : k + 1]
        scaled = jnp.where(lane == k, 1.0 + recip, row * recip)
        for t in range(t0, HALF // 8):
            col = tiles[t][:, k : k + 1]
            if t == t0:
                if s0 == 7:
                    continue
                col = jnp.where(sub > s0, col, 0.0)
            tiles[t] = tiles[t] - col * scaled
    work = jnp.concatenate(tiles, axis=0)
    pivots = jnp.sum(jnp.where(on_diag, work, 0.0), axis=1, keepdims=True)
    unit = jnp.where(on_diag, 1.0, jnp.where(col_at < row_at, work, 0.0))
    return unit * lax.rsqrt(pivots) * scale_row


def factor_kernel(core_ref, main_ref, extra_ref, other_ref, out_ref):
    row_at, col_at = square_iotas()
    eye = (row_at == col_at).astype(jnp.float32)
    first_core = core_ref[0] == 0
    other = other_ref[:HALF]
    cross = jnp.where(first_core, main_ref[...], other)
    merged = jnp.where(first_core, other, main_ref[...])
    extra = jnp.where(first_core, extra_ref[...], other_ref[HALF:])
    merged_t = merged.T
    first = jnp.where(col_at <= row_at, merged, merged_t) + eye
    second = jnp.where(col_at > row_at, merged, merged_t)
    second = jnp.where(col_at == row_at, extra[0:1], second) + eye
    moment1 = extra[1:2]
    moment2 = extra[2:3]
    inv1 = invert_factor(first)
    low = dot_nt(cross, inv1)
    inv2 = invert_factor(second - dot_nt(low, low))
    inv21 = -dot_nn(inv2, dot_nn(low, inv1))
    inner1 = jnp.sum(inv1 * moment1, axis=1, keepdims=True)
    inner2 = jnp.sum(inv21 * moment1 + inv2 * moment2, axis=1, keepdims=True)
    coef1 = jnp.sum(inv1 * inner1 + inv21 * inner2, axis=0, keepdims=True)
    coef2 = jnp.sum(inv2 * inner2, axis=0, keepdims=True)
    spread1 = jnp.sum(inv1 * inv1 + inv21 * inv21, axis=0, keepdims=True)
    spread2 = jnp.sum(inv2 * inv2, axis=0, keepdims=True)
    extra_out = jnp.concatenate(
        [
            jnp.sum(inv2 * eye, axis=0, keepdims=True),
            coef1 / jnp.sqrt(spread1),
            coef2 / jnp.sqrt(spread2),
            jnp.zeros((5, HALF), jnp.float32),
        ],
        axis=0,
    )
    merged_out = jnp.where(col_at <= row_at, inv1, inv2.T)
    main_out = jnp.where(first_core, inv21, merged_out)
    for p in range(out_ref.shape[0]):
        out_ref[p, :HALF] = main_out
        out_ref[p, HALF:] = extra_out


def factor_of(core, main, extra, other):
    vmem = pl.BlockSpec(memory_space=pltpu.VMEM)
    return pl.pallas_call(
        factor_kernel,
        out_shape=jax.ShapeDtypeStruct((HEADS, PACKED, HALF), jnp.float32),
        in_specs=[pl.BlockSpec(memory_space=pltpu.SMEM), vmem, vmem, vmem],
        out_specs=vmem,
        name="factor",
    )(core, main, extra, other)


def lever_kernel(
    lever_scale, factor_scale, head_ref, place_ref, table_ref, id_ref, own_ref, other_ref, feat_ref,
    out_ref, score_ref, piece_ref, low_ref, full_ref,
):
    step = pl.program_id(0)
    heads = low_ref.shape[0]
    piece_rows = piece_ref.shape[1]

    @pl.when(step == 0)
    def _():
        first_core = place_ref[1] == 0
        row_at, col_at = square_iotas()
        own_rows = pl.ds(pl.multiple_of(place_ref[0] * piece_rows, piece_rows), piece_rows)
        for h in range(heads):
            own = own_ref[h, :HALF]
            other = other_ref[h, :HALF]
            merged = jnp.where(first_core, other, own)
            second = jnp.where(col_at > row_at, merged, 0.0).T
            second = jnp.where(col_at == row_at, own_ref[h, HALF : HALF + 1], second)
            full_ref[h, :HALF, :HALF] = jnp.where(col_at <= row_at, merged, 0.0)
            full_ref[h, :HALF, HALF:] = jnp.zeros((HALF, HALF), jnp.float32)
            full_ref[h, HALF:, :HALF] = jnp.where(first_core, own, other)
            full_ref[h, HALF:, HALF:] = second
            low_ref[h] = full_ref[h].astype(jnp.bfloat16)
            score_ref[h : h + 1, :HALF] = own_ref[h, HALF + 1 : HALF + 2]
            score_ref[h : h + 1, HALF:] = own_ref[h, HALF + 2 : HALF + 3]
            piece_ref[h] = full_ref[h, own_rows, :] * factor_scale

    weight = row_weights(table_ref[...], id_ref[...])
    projected = lax.dot_general(
        low_ref[head_ref[step]],
        feat_ref[...],
        (((1,), (1,)), ((), ())),
        preferred_element_type=jnp.float32,
    )
    squares = jnp.sum(projected * projected, axis=0, keepdims=True)
    squares = jnp.concatenate(
        [squares[:, s * HALF : (s + 1) * HALF] for s in range(BLK // HALF)], axis=0
    )
    out_ref[...] = weight * squares * lever_scale


def lever_of(
    block_heads, place, table, ids, own, other, features, lever_scale, factor_scale, piece_rows
):
    rows, width = features.shape
    blocks = rows // BLK
    return pl.pallas_call(
        functools.partial(lever_kernel, lever_scale, factor_scale),
        out_shape=(
            jax.ShapeDtypeStruct((rows // HALF, HALF), jnp.float32),
            jax.ShapeDtypeStruct((HEADS, width), jnp.float32),
            jax.ShapeDtypeStruct((HEADS, piece_rows, width), jnp.float32),
        ),
        grid_spec=pltpu.PrefetchScalarGridSpec(
            num_scalar_prefetch=2,
            grid=(blocks,),
            in_specs=[
                pl.BlockSpec((1, HALF), lambda b, h, o: (0, 0)),
                pl.BlockSpec((BLK // HALF, HALF), lambda b, h, o: (b, 0)),
                pl.BlockSpec((HEADS, PACKED, HALF), lambda b, h, o: (0, 0, 0)),
                pl.BlockSpec((HEADS, PACKED, HALF), lambda b, h, o: (0, 0, 0)),
                pl.BlockSpec((BLK, width), lambda b, h, o: (b, 0)),
            ],
            out_specs=(
                pl.BlockSpec((BLK // HALF, HALF), lambda b, h, o: (b, 0)),
                pl.BlockSpec((HEADS, width), lambda b, h, o: (0, 0)),
                pl.BlockSpec((HEADS, piece_rows, width), lambda b, h, o: (0, 0, 0)),
            ),
            scratch_shapes=[
                pltpu.VMEM((HEADS, width, width), jnp.bfloat16),
                pltpu.VMEM((HEADS, width, width), jnp.float32),
            ],
        ),
        name="lever",
    )(block_heads, place, table, ids, own, other, features)


def swap_cores(value):
    return lax.ppermute(value, "c", [(0, 1), (1, 0)])


def exchange(value, axes):
    return lax.all_to_all(value, axes, 0, 0, tiled=True)


def local(features, targets, station_ids, lead_heads, station_weight):
    row_count, feat_width = features.shape
    block_count = row_count // BLK
    pieces = lax.axis_size(("y", "zl", "c"))
    total_rows = row_count * lax.axis_size(PLANE + COLUMN + ("c",))
    core = lax.axis_index("c").astype(jnp.int32)
    piece_at = lax.axis_index(("y", "zl", "c")).astype(jnp.int32)
    block_heads = lead_heads.reshape(block_count, BLK)[:, 0]
    ids = station_ids.reshape(row_count // HALF, HALF)
    target_rows = targets.astype(jnp.float32).reshape(row_count // HALF, HALF)
    core_at = core.reshape(1)
    place = jnp.stack([piece_at, core])

    keep, send = gram_of(block_heads, core_at, station_weight, ids, target_rows, features)
    chip = keep + swap_cores(send)
    column_rows = HALF // COLUMN_SIZE
    parts = whole_call(
        plane_sum_kernel,
        jax.ShapeDtypeStruct((COLUMN_SIZE, column_rows + 8, HALF), jnp.float32),
        "plane_sum",
        exchange(chip, PLANE),
    )
    summed, extra = whole_call(
        column_sum_kernel,
        (
            jax.ShapeDtypeStruct((COLUMN_SIZE, column_rows, HALF), jnp.float32),
            jax.ShapeDtypeStruct((8, HALF), jnp.float32),
        ),
        "column_sum",
        exchange(parts, COLUMN),
    )
    main = exchange(summed, COLUMN).reshape(HALF, HALF)
    other = swap_cores(jnp.concatenate([main, extra], axis=0))
    own_inverses = exchange(factor_of(core_at, main, extra, other), PLANE)
    other_inverses = swap_cores(own_inverses)
    leverage, zscores, inverse_factor = lever_of(
        block_heads,
        place,
        station_weight,
        ids,
        own_inverses,
        other_inverses,
        features,
        total_rows / (HEADS * feat_width),
        math.sqrt(total_rows / HEADS),
        feat_width // pieces,
    )
    return (leverage.reshape(row_count), zscores, inverse_factor)


def solution(mesh):
    grid = Mesh(mesh.devices.reshape(4, 2, 4, 4, 2), ("x", "zh", "y", "zl", "c"))
    rows = ("x", "zh", "y", "zl", "c")
    return jax.shard_map(
        local,
        mesh=grid,
        in_specs=(P(rows, None), P(rows), P(rows), P(rows), P(("x", "zh"), None)),
        out_specs=(P(rows), P(), P(None, ("y", "zl", "c"), None)),
        check_vma=False,
    )
```

time: 1240 us -> 152 us (0.12)
  other arithmetic: 875 us -> 4.11 us
  waiting for transfers between devices: 184 us -> 5.22 us
  Pallas kernels: 0 us -> 59.4 us
  matrix products: 50.1 us -> 0 us
  local copies, waits for them, and re-layouts: 28 us -> 3.13 us
  between operations: 14.8 us -> 0.65 us
  blocking collectives: 82 us -> 69.5 us
    another operation x13 -> x1, other arithmetic: 856 us -> 0.66 us  [local(): place = jnp.stack([piece_at, core])]
    psum x1 -> x0, waiting for transfers between devices: 184 us -> none  [local(): gram_payload, moment = lax.psum((gram_payload, moment), ('station', 'tm'))]
    psum x1 -> x0, blocking collectives: 82 us -> none  [local(): gram_payload, moment = lax.psum((gram_payload, moment), ('station', 'tm'))]
    all_to_all x0 -> x4, blocking collectives: none -> 69.5 us  [exchange(): return lax.all_to_all(value, axes, 0, 0, tiled=True)]
    pallas_call x0 -> x5, Pallas kernels: none -> 59.4 us  [the longest x1 25 us: factor_of(): pl.pallas_call(factor_kernel, out_shape=jax.ShapeDtypeStruct((HEADS, PACK...]
    dot_general x9 -> x0, matrix products: 38.4 us -> none  [the longest x1 8.25 us: local(): jnp.einsum('bri,brj->bij', weight_blocks, feat_blocks, preferred_element_...]
  transfers between devices with their start and end apart: 1 -> 3, of which waited for: 1 -> 3; matrix products, arithmetic and copies ran while one was open for 0% -> 0% of each run, Pallas kernels for 0% -> 0%
where the time goes in v1:
time: 152 us; the launch traced here: 151 us
  blocking collectives  69.5 us (46%)
  Pallas kernels  59.4 us (39%)
  starting transfers between devices  8.8 us (6%)
  waiting for transfers between devices  5.22 us (3%)
  other arithmetic  4.11 us (3%)
  local copies, waits for them, and re-layouts  3.13 us (2%)
    all_to_all x4, blocking collectives, exchange(): return lax.all_to_all(value, axes, 0, 0, tiled=True)  69.5 us
    pallas_call x1, Pallas kernels, factor_of(): pl.pallas_call(factor_kernel, out_shape=jax.ShapeDtypeStruct((HEADS, PACK...  25 us
    pallas_call x1, Pallas kernels, gram_of(): pl.pallas_call(gram_kernel, out_shape=(half, half), grid_spec=pltpu.Prefe...  16 us
    pallas_call x1, Pallas kernels, lever_of(): pl.pallas_call(functools.partial(lever_kernel, lever_scale, factor_scale)...  15 us
    ppermute x3, starting transfers between devices, swap_cores(): return lax.ppermute(value, 'c', [(0, 1), (1, 0)])  8.8 us
    ppermute x3, waiting for transfers between devices, swap_cores(): return lax.ppermute(value, 'c', [(0, 1), (1, 0)])  5.22 us
    pallas_call x2, Pallas kernels, whole_call(): pl.pallas_call(kernel, out_shape=out_shape, in_specs=[vmem] * len(args),...  3.48 us
  transfers between devices with their start and end apart: 3, of which 3 were waited for; matrix products, arithmetic and copies ran while one was open for 0% of the time, Pallas kernels for 0%

profile of v1, /device:TPU:1, one launch (start us, length us, event | category | flops | bytes accessed | tf_op | source)
XLA Modules:
  0.0 150.8 jit_solution(11242651469722814268)
XLA Ops:
  0.6 1.4 bitcast_convert_fusion.target_ref
  2.0 0.9 reshape.24
  2.9 0.6 slice_reduce_fusion.head_ref
  3.5 16.0 %gram.1 = (f32[16,136,128]{2,1,0:T(8,128)}, f32[16,136,128]{2,1,0:T(8,128)}) custom-call(s32[16]{0:T(128)} %slice_reduce_fusion.head_ref, s32[1]{0:T(128)} %bitcast.1.core_ref, f32[1,128]{1,0:T(1,128)} %table_ref.3, s32[128,128]{1,0:T(8,128)} %bitcast.10, f32[128,128]{1,0:T(8,128)} %bitcast_convert_fusion.target_ref, bf16[16384,256]{1,0:T(8,128)(2,1)} %feat_ref.3), custom_call_target="tpu_custom_call" | custom-call | flops 2147483648 | bytes 8388608 | tf_op jit(solution)/shard_map/gram/pallas_call | solution.py:95
  19.5 3.2 %collective-permute-start = (f32[16,136,128]{2,1,0:T(8,128)}, f32[16,136,128]{2,1,0:T(8,128)S(1)}, u32[]{:S(2)}, u32[]{:S(2)}) collective-permute-start(f32[16,136,128]{2,1,0:T(8,128)} %get-tuple-element.11), channel_id=1, source_target_pairs={{0,1},{1,0},{2,3},{3,2},{4,5},{5,4},{6,7},{7,6},{8,9},{9,8},{10,11... | collective-permute-start | bytes 3342344 | tf_op jit(solution)/shard_map/ppermute | solution.py:307
  22.7 2.6 %collective-permute-done = f32[16,136,128]{2,1,0:T(8,128)S(1)} collective-permute-done((f32[16,136,128]{2,1,0:T(8,128)}, f32[16,136,128]{2,1,0:T(8,128)S(1)}, u32[]{:S(2)}, u32[]{:S(2)}) %collective-permute-start) | collective-permute-done | bytes 1114144 | tf_op jit(solution)/shard_map/ppermute | solution.py:307
  25.3 1.4 add.11
  26.7 22.1 %all_to_all.20.part_ref = f32[16,136,128]{2,1,0:T(8,128)} all-to-all(f32[16,136,128]{2,1,0:T(8,128)S(1)} %add.11), channel_id=1, replica_groups=mesh['x'=4,'zh'=2,'y'=4,'zl'=4,'c'=2] {'x','y'}, dimensions={0} | all-to-all | bytes 2228224 | tf_op jit(solution)/shard_map/all_to_all | solution.py:311
  48.8 1.9 %plane_sum.1 = f32[8,24,128]{2,1,0:T(8,128)} custom-call(f32[16,136,128]{2,1,0:T(8,128)} %all_to_all.20.part_ref), custom_call_target="tpu_custom_call" | custom-call | tf_op jit(solution)/shard_map/plane_sum/pallas_call | solution.py:144
  50.7 16.0 %all_to_all.21.part_ref = f32[8,24,128]{2,1,0:T(8,128)} all-to-all(f32[8,24,128]{2,1,0:T(8,128)} %plane_sum.1), channel_id=1, replica_groups=mesh['x'=4,'zh'=2,'y'=4,'zl'=4,'c'=2] {'zh','zl'}, dimensions={0} | all-to-all | bytes 196608 | tf_op jit(solution)/shard_map/all_to_all | solution.py:311
  66.7 1.5 %column_sum.1 = (f32[8,16,128]{2,1,0:T(8,128)}, f32[8,128]{1,0:T(8,128)}) custom-call(f32[8,24,128]{2,1,0:T(8,128)} %all_to_all.21.part_ref), custom_call_target="tpu_custom_call" | custom-call | tf_op jit(solution)/shard_map/column_sum/pallas_call | solution.py:144
  68.2 10.5 %all_to_all.22 = f32[8,16,128]{2,1,0:T(8,128)S(1)} all-to-all(f32[8,16,128]{2,1,0:T(8,128)} %get-tuple-element.12), channel_id=1, replica_groups=mesh['x'=4,'zh'=2,'y'=4,'zl'=4,'c'=2] {'zh','zl'}, dimensions={0} | all-to-all | bytes 131072 | tf_op jit(solution)/shard_map/all_to_all | solution.py:311
  78.7 0.0 copy-start.2
  78.7 0.7 pad_maximum_fusion
  79.4 4.1 %collective-permute-start.1 = (f32[136,128]{1,0:T(8,128)S(1)}, f32[136,128]{1,0:T(8,128)S(1)}, u32[]{:S(2)}, u32[]{:S(2)}) collective-permute-start(f32[136,128]{1,0:T(8,128)S(1)} %pad_maximum_fusion), channel_id=1, source_target_pairs={{0,1},{1,0},{2,3},{3,2},{4,5},{5,4},{6,7},{7,6},{8,9},{9,8},{10,11... | collective-permute-start | bytes 208904 | tf_op jit(solution)/shard_map/ppermute | solution.py:307
  83.5 0.9 collective-permute-done.1.other_ref
  84.5 0.0 copy-done.2
  84.5 0.0 copy-start.3
  84.5 0.6 copy-done.3
  85.1 25.0 %factor.1 = f32[16,136,128]{2,1,0:T(8,128)} custom-call(s32[1]{0:T(128)} %bitcast.1.core_ref, f32[128,128]{1,0:T(8,128)} %bitcast.9, f32[8,128]{1,0:T(8,128)} %get-tuple-element.13.extra_ref, f32[136,128]{1,0:T(8,128)} %copy-done.3), custom_call_target="tpu_custom_call" | custom-call | tf_op jit(solution)/shard_map/factor/pallas_call | solution.py:219
  110.1 21.0 %all_to_all.23.own_ref = f32[16,136,128]{2,1,0:T(8,128)S(1)} all-to-all(f32[16,136,128]{2,1,0:T(8,128)} %factor.1), channel_id=1, replica_groups=mesh['x'=4,'zh'=2,'y'=4,'zl'=4,'c'=2] {'x','y'}, dimensions={0} | all-to-all | bytes 2228224 | tf_op jit(solution)/shard_map/all_to_all | solution.py:311
  131.1 0.0 copy-start
  131.1 1.4 collective-permute-start.2
  132.5 0.7 pad_add_fusion.place_ref
  133.1 1.7 %collective-permute-done.2.other_ref = f32[16,136,128]{2,1,0:T(8,128)S(1)} collective-permute-done((f32[16,136,128]{2,1,0:T(8,128)S(1)}, f32[16,136,128]{2,1,0:T(8,128)S(1)}, u32[]{:S(2)}, u32[]{:S(2)}) %collective-permute-start.2) | collective-permute-done | bytes 1114144 | tf_op jit(solution)/shard_map/ppermute | solution.py:307
  134.9 0.0 copy-done
  134.9 0.0 copy-start.1
  134.9 1.0 copy-done.1
  135.9 15.0 %lever.1 = (f32[128,128]{1,0:T(8,128)}, f32[16,256]{1,0:T(8,128)}, f32[16,8,256]{2,1,0:T(8,128)}) custom-call(s32[16]{0:T(128)} %slice_reduce_fusion.head_ref, s32[2]{0:T(128)} %pad_add_fusion.place_ref, f32[1,128]{1,0:T(1,128)} %table_ref.3, s32[128,128]{1,0:T(8,128)} %bitcast.11, f32[16,136,128]{2,1,0:T(8,128)} %copy-done, f32[16,136,128]{2,1,0:T(8,128)} %copy-done.1, ...), custom_call_target="tpu_custom_call" | custom-call | tf_op jit(solution)/shard_map/lever/pallas_call | solution.py:275
Async XLA Ops:
  19.5 5.8 %collective-permute-start = (f32[16,136,128]{2,1,0:T(8,128)}, f32[16,136,128]{2,1,0:T(8,128)S(1)}, u32[]{:S(2)}, u32[]{:S(2)}) collective-permute-start(f32[16,136,128]{2,1,0:T(8,128)} %get-tuple-element.11), channel_id=1, source_target_pairs={{0,1},{1,0},{2,3},{3,2},{4,5},{5,4},{6,7},{7,6},{8,9},{9,8},{10,11... | collective-permute-start | bytes 3342344 | tf_op jit(solution)/shard_map/ppermute | solution.py:307
  78.7 5.8 %copy-start.2 = (f32[8,16,128]{2,1,0:T(8,128)}, f32[8,16,128]{2,1,0:T(8,128)S(1)}, u32[]{:S(2)}) copy-start(f32[8,16,128]{2,1,0:T(8,128)S(1)} %all_to_all.22) | copy-start | bytes 196612
  79.4 5.1 %collective-permute-start.1 = (f32[136,128]{1,0:T(8,128)S(1)}, f32[136,128]{1,0:T(8,128)S(1)}, u32[]{:S(2)}, u32[]{:S(2)}) collective-permute-start(f32[136,128]{1,0:T(8,128)S(1)} %pad_maximum_fusion), channel_id=1, source_target_pairs={{0,1},{1,0},{2,3},{3,2},{4,5},{5,4},{6,7},{7,6},{8,9},{9,8},{10,11... | collective-permute-start | bytes 208904 | tf_op jit(solution)/shard_map/ppermute | solution.py:307
  84.5 0.6 copy-start.3
  131.1 3.8 %copy-start = (f32[16,136,128]{2,1,0:T(8,128)}, f32[16,136,128]{2,1,0:T(8,128)S(1)}, u32[]{:S(2)}) copy-start(f32[16,136,128]{2,1,0:T(8,128)S(1)} %all_to_all.23.own_ref) | copy-start | bytes 3342340
  131.1 3.8 %collective-permute-start.2 = (f32[16,136,128]{2,1,0:T(8,128)S(1)}, f32[16,136,128]{2,1,0:T(8,128)S(1)}, u32[]{:S(2)}, u32[]{:S(2)}) collective-permute-start(f32[16,136,128]{2,1,0:T(8,128)S(1)} %all_to_all.23.own_ref), channel_id=1, source_target_pairs={{0,1},{1,0},{2,3},{3,2},{4,5},{5,4},{6,7},{7,6},{8,9},{9,8},{10,11... | collective-permute-start | bytes 3342344 | tf_op jit(solution)/shard_map/ppermute | solution.py:307
  134.9 1.0 copy-start.1

commit v2 on v1

v2 whole, which is shorter than its diff:
```python
import functools
import math

import jax
import jax.numpy as jnp
from jax import lax
from jax.experimental import pallas as pl
from jax.experimental.pallas import tpu as pltpu
from jax.sharding import Mesh, PartitionSpec as P

HEADS = 16
BLK = 1024
PER_STEP = 4
HALF = 128
PACKED = HALF + 8
EXACT = lax.Precision.HIGHEST
PLANE = ("x", "y")
COLUMN = ("zh", "zl")
SMALL = 8 << 20
WIDE = 56 << 20
LARGE = 51 << 20


def dot_nn(a, b):
    return lax.dot_general(
        a, b, (((1,), (0,)), ((), ())), precision=EXACT, preferred_element_type=jnp.float32
    )


def dot_nt(a, b):
    return lax.dot_general(
        a, b, (((1,), (1,)), ((), ())), precision=EXACT, preferred_element_type=jnp.float32
    )


def square_iotas():
    row_at = lax.broadcasted_iota(jnp.int32, (HALF, HALF), 0)
    col_at = lax.broadcasted_iota(jnp.int32, (HALF, HALF), 1)
    return row_at, col_at


def row_weights(table, ids):
    return jnp.take_along_axis(jnp.broadcast_to(table, ids.shape), ids, axis=1)


def gram_kernel(
    head_ref, core_ref, table_ref, id_ref, target_ref, feat_ref,
    keep_ref, send_ref, total_ref, moment_ref, pair_ref,
):
    step = pl.program_id(0)
    heads = total_ref.shape[0]

    @pl.when(step == 0)
    def _():
        total_ref[...] = jnp.zeros_like(total_ref)
        moment_ref[...] = jnp.zeros_like(moment_ref)

    table = table_ref[...]
    sublanes = BLK // HALF
    for i in range(PER_STEP):
        lines = slice(i * sublanes, (i + 1) * sublanes)
        feats = feat_ref[i * BLK : (i + 1) * BLK]
        weight = row_weights(table, id_ref[lines])
        target = target_ref[lines].astype(jnp.float32)
        head = head_ref[(step * PER_STEP + i) * BLK]
        flipped = feats.T
        pieces = []
        for s in range(sublanes):
            piece = flipped[:, s * HALF : (s + 1) * HALF].astype(jnp.float32)
            pieces.append((piece * weight[s : s + 1, :]).astype(jnp.bfloat16))
        weighted = jnp.concatenate(pieces, axis=1)
        total_ref[head] += jnp.dot(weighted, feats, preferred_element_type=jnp.float32)
        target_row = jnp.concatenate([target[s : s + 1, :] for s in range(sublanes)], axis=1)
        target_row = jnp.broadcast_to(target_row, (8, BLK)).astype(jnp.bfloat16)
        moment_ref[head] += lax.dot_general(
            target_row, weighted, (((1,), (1,)), ((), ())), preferred_element_type=jnp.float32
        )

    @pl.when(step == pl.num_programs(0) - 1)
    def _():
        core = core_ref[0]
        row_at, col_at = square_iotas()
        pair_ref[1, HALF:] = jnp.zeros((8, HALF), jnp.float32)
        for h in range(heads):
            second = total_ref[h, HALF:, HALF:]
            diag = jnp.sum(jnp.where(row_at == col_at, second, 0.0), axis=0, keepdims=True)
            moment = moment_ref[h, 0:1]
            pair_ref[0, :HALF] = total_ref[h, HALF:, :HALF]
            pair_ref[0, HALF:] = jnp.concatenate(
                [diag, moment[:, :HALF], moment[:, HALF:], jnp.zeros((5, HALF), jnp.float32)],
                axis=0,
            )
            pair_ref[1, :HALF] = jnp.where(col_at <= row_at, total_ref[h, :HALF, :HALF], second)
            keep_ref[h] = pair_ref[core]
            send_ref[h] = pair_ref[1 - core]


def gram_of(lead_heads, core, table, ids, targets, features):
    rows, width = features.shape
    blocks = rows // BLK
    half = jax.ShapeDtypeStruct((HEADS, PACKED, HALF), jnp.float32)
    half_spec = pl.BlockSpec((HEADS, PACKED, HALF), lambda b, h, c: (0, 0, 0))
    return pl.pallas_call(
        gram_kernel,
        out_shape=(half, half),
        grid_spec=pltpu.PrefetchScalarGridSpec(
            num_scalar_prefetch=2,
            grid=(blocks // PER_STEP,),
            in_specs=[
                pl.BlockSpec((1, HALF), lambda b, h, c: (0, 0)),
                pl.BlockSpec((PER_STEP * BLK // HALF, HALF), lambda b, h, c: (b, 0)),
                pl.BlockSpec((PER_STEP * BLK // HALF, HALF), lambda b, h, c: (b, 0)),
                pl.BlockSpec((PER_STEP * BLK, width), lambda b, h, c: (b, 0)),
            ],
            out_specs=(half_spec, half_spec),
            scratch_shapes=[
                pltpu.VMEM((HEADS, width, width), jnp.float32),
                pltpu.VMEM((HEADS, 8, width), jnp.float32),
                pltpu.VMEM((2, PACKED, HALF), jnp.float32),
            ],
        ),
        cost_estimate=pl.CostEstimate(
            flops=2 * rows * width * width, bytes_accessed=2 * rows * width, transcendentals=0
        ),
        compiler_params=pltpu.CompilerParams(vmem_limit_bytes=WIDE),
        name="gram",
    )(lead_heads, core, table, ids, targets, features)


def plane_sum_kernel(part_ref, out_ref):
    total = part_ref[0]
    for p in range(1, part_ref.shape[0]):
        total = total + part_ref[p]
    out_ref[...] = total


def column_sum_kernel(*refs):
    place_ref, *part_refs, out_ref, ordered_ref = refs
    count = len(part_refs)
    for k in range(count):
        ordered_ref[lax.rem(place_ref[0] + k, count)] = part_refs[k][...]
    total = ordered_ref[0]
    for k in range(1, count):
        total = total + ordered_ref[k]
    out_ref[...] = total


def column_sum(place, parts):
    vmem = pl.BlockSpec(memory_space=pltpu.VMEM)
    shape = parts[0].shape
    return pl.pallas_call(
        column_sum_kernel,
        out_shape=jax.ShapeDtypeStruct(shape, jnp.float32),
        in_specs=[pl.BlockSpec(memory_space=pltpu.SMEM)] + [vmem] * len(parts),
        out_specs=vmem,
        scratch_shapes=[pltpu.VMEM((len(parts),) + shape, jnp.float32)],
        compiler_params=pltpu.CompilerParams(vmem_limit_bytes=SMALL),
        name="column_sum",
    )(place, *parts)


def whole_call(kernel, out_shape, name, *args):
    vmem = pl.BlockSpec(memory_space=pltpu.VMEM)
    outs = jax.tree.map(lambda _: vmem, out_shape)
    return pl.pallas_call(
        kernel,
        out_shape=out_shape,
        in_specs=[vmem] * len(args),
        out_specs=outs,
        compiler_params=pltpu.CompilerParams(vmem_limit_bytes=SMALL),
        name=name,
    )(*args)


def invert_factor(sym):
    tiles = [sym[8 * t : 8 * t + 8, :] for t in range(HALF // 8)]
    lane = lax.broadcasted_iota(jnp.int32, (8, HALF), 1)
    sub = lax.broadcasted_iota(jnp.int32, (8, HALF), 0)
    rows = []
    for p in range(HALF // 8):
        inside = (lane >= 8 * p) & (lane < 8 * p + 8)
        cols = [jnp.broadcast_to(tiles[p][:, 8 * p + j : 8 * p + j + 1], (8, HALF)) for j in range(8)]
        below = {
            t: [jnp.broadcast_to(tiles[t][:, 8 * p + j : 8 * p + j + 1], (8, HALF)) for j in range(8)]
            for t in range(p + 1, HALF // 8)
        }
        panel = jnp.where(inside, jnp.where(lane == 8 * p + sub, 1.0, 0.0), tiles[p])
        for t in below:
            tiles[t] = jnp.where(inside, 0.0, tiles[t])
        pivots = jnp.ones((8, HALF), jnp.float32)
        for k in range(8):
            pivot = jnp.broadcast_to(cols[k][k : k + 1], (8, HALF))
            recip = 1.0 / pivot
            pivots = jnp.where(sub == k, pivot, pivots)
            across = [jnp.broadcast_to(cols[j][k : k + 1], (8, HALF)) for j in range(k + 1, 8)]
            row = jnp.broadcast_to(panel[k : k + 1], (8, HALF))
            if k < 7:
                scaled = jnp.where(sub > k, cols[k] * recip, 0.0)
                for j in range(k + 1, 8):
                    cols[j] = cols[j] - scaled * across[j - k - 1]
                panel = panel - scaled * row
            for t in below:
                scaled = below[t][k] * recip
                for j in range(k + 1, 8):
                    below[t][j] = below[t][j] - scaled * across[j - k - 1]
                tiles[t] = tiles[t] - scaled * row
        rows.append(jnp.where(lane <= 8 * p + sub, panel, 0.0) * lax.rsqrt(pivots))
    return jnp.concatenate(rows, axis=0)


def factor_kernel(core_ref, own_ref, other_ref, out_ref):
    row_at, col_at = square_iotas()
    eye = (row_at == col_at).astype(jnp.float32)
    first_core = core_ref[0] == 0
    own = own_ref[:HALF]
    other = other_ref[:HALF]
    cross = jnp.where(first_core, own, other)
    merged = jnp.where(first_core, other, own)
    extra = jnp.where(first_core, own_ref[HALF:], other_ref[HALF:])
    merged_t = merged.T
    first = jnp.where(col_at <= row_at, merged, merged_t) + eye
    second = jnp.where(col_at > row_at, merged, merged_t)
    second = jnp.where(col_at == row_at, extra[0:1], second) + eye
    moment1 = extra[1:2]
    moment2 = extra[2:3]
    inv1 = invert_factor(first)
    low = dot_nt(cross, inv1)
    inv2 = invert_factor(second - dot_nt(low, low))
    inv21 = -dot_nn(inv2, dot_nn(low, inv1))
    inner1 = jnp.sum(inv1 * moment1, axis=1, keepdims=True)
    inner2 = jnp.sum(inv21 * moment1 + inv2 * moment2, axis=1, keepdims=True)
    coef1 = jnp.sum(inv1 * inner1 + inv21 * inner2, axis=0, keepdims=True)
    coef2 = jnp.sum(inv2 * inner2, axis=0, keepdims=True)
    spread1 = jnp.sum(inv1 * inv1 + inv21 * inv21, axis=0, keepdims=True)
    spread2 = jnp.sum(inv2 * inv2, axis=0, keepdims=True)
    extra_out = jnp.concatenate(
        [
            jnp.sum(inv2 * eye, axis=0, keepdims=True),
            coef1 / jnp.sqrt(spread1),
            coef2 / jnp.sqrt(spread2),
            jnp.zeros((5, HALF), jnp.float32),
        ],
        axis=0,
    )
    merged_out = jnp.where(col_at <= row_at, inv1, inv2.T)
    main_out = jnp.where(first_core, inv21, merged_out)
    for p in range(out_ref.shape[0]):
        out_ref[p, :HALF] = main_out
        out_ref[p, HALF:] = extra_out


def factor_of(core, own, other):
    vmem = pl.BlockSpec(memory_space=pltpu.VMEM)
    return pl.pallas_call(
        factor_kernel,
        out_shape=jax.ShapeDtypeStruct((HEADS, PACKED, HALF), jnp.float32),
        in_specs=[pl.BlockSpec(memory_space=pltpu.SMEM), vmem, vmem],
        out_specs=vmem,
        compiler_params=pltpu.CompilerParams(vmem_limit_bytes=SMALL),
        name="factor",
    )(core, own, other)


def lever_kernel(
    lever_scale, factor_scale, head_ref, place_ref, table_ref, id_ref, own_ref, other_ref, feat_ref,
    out_ref, score_ref, piece_ref, low_ref, full_ref,
):
    step = pl.program_id(0)
    heads = low_ref.shape[0]
    piece_rows = piece_ref.shape[1]

    @pl.when(step == 0)
    def _():
        first_core = place_ref[1] == 0
        row_at, col_at = square_iotas()
        own_rows = pl.ds(pl.multiple_of(place_ref[0] * piece_rows, piece_rows), piece_rows)
        for h in range(heads):
            own = own_ref[h, :HALF]
            other = other_ref[h, :HALF]
            merged = jnp.where(first_core, other, own)
            second = jnp.where(col_at > row_at, merged, 0.0).T
            second = jnp.where(col_at == row_at, own_ref[h, HALF : HALF + 1], second)
            full_ref[h, :HALF, :HALF] = jnp.where(col_at <= row_at, merged, 0.0)
            full_ref[h, :HALF, HALF:] = jnp.zeros((HALF, HALF), jnp.float32)
            full_ref[h, HALF:, :HALF] = jnp.where(first_core, own, other)
            full_ref[h, HALF:, HALF:] = second
            low_ref[h] = full_ref[h].astype(jnp.bfloat16)
            score_ref[h : h + 1, :HALF] = own_ref[h, HALF + 1 : HALF + 2]
            score_ref[h : h + 1, HALF:] = own_ref[h, HALF + 2 : HALF + 3]
            piece_ref[h] = full_ref[h, own_rows, :] * factor_scale

    table = table_ref[...]
    sublanes = BLK // HALF
    for i in range(PER_STEP):
        lines = slice(i * sublanes, (i + 1) * sublanes)
        weight = row_weights(table, id_ref[lines])
        projected = lax.dot_general(
            low_ref[head_ref[(step * PER_STEP + i) * BLK]],
            feat_ref[i * BLK : (i + 1) * BLK],
            (((1,), (1,)), ((), ())),
            preferred_element_type=jnp.float32,
        )
        squares = jnp.sum(projected * projected, axis=0, keepdims=True)
        squares = jnp.concatenate(
            [squares[:, s * HALF : (s + 1) * HALF] for s in range(sublanes)], axis=0
        )
        out_ref[lines] = weight * squares * lever_scale


def lever_of(
    lead_heads, place, table, ids, own, other, features, lever_scale, factor_scale, piece_rows
):
    rows, width = features.shape
    blocks = rows // BLK
    return pl.pallas_call(
        functools.partial(lever_kernel, lever_scale, factor_scale),
        out_shape=(
            jax.ShapeDtypeStruct((rows // HALF, HALF), jnp.float32),
            jax.ShapeDtypeStruct((HEADS, width), jnp.float32),
            jax.ShapeDtypeStruct((HEADS, piece_rows, width), jnp.float32),
        ),
        grid_spec=pltpu.PrefetchScalarGridSpec(
            num_scalar_prefetch=2,
            grid=(blocks // PER_STEP,),
            in_specs=[
                pl.BlockSpec((1, HALF), lambda b, h, o: (0, 0)),
                pl.BlockSpec((PER_STEP * BLK // HALF, HALF), lambda b, h, o: (b, 0)),
                pl.BlockSpec((HEADS, PACKED, HALF), lambda b, h, o: (0, 0, 0)),
                pl.BlockSpec((HEADS, PACKED, HALF), lambda b, h, o: (0, 0, 0)),
                pl.BlockSpec((PER_STEP * BLK, width), lambda b, h, o: (b, 0)),
            ],
            out_specs=(
                pl.BlockSpec((PER_STEP * BLK // HALF, HALF), lambda b, h, o: (b, 0)),
                pl.BlockSpec((HEADS, width), lambda b, h, o: (0, 0)),
                pl.BlockSpec((HEADS, piece_rows, width), lambda b, h, o: (0, 0, 0)),
            ),
            scratch_shapes=[
                pltpu.VMEM((HEADS, width, width), jnp.bfloat16),
                pltpu.VMEM((HEADS, width, width), jnp.float32),
            ],
        ),
        compiler_params=pltpu.CompilerParams(vmem_limit_bytes=LARGE),
        name="lever",
    )(lead_heads, place, table, ids, own, other, features)


def swap_cores(value):
    return lax.ppermute(value, "c", [(0, 1), (1, 0)])


def around_column(value):
    count = lax.axis_size(COLUMN)
    up = [(i, (i + 1) % count) for i in range(count)]
    down = [(i, (i - 1) % count) for i in range(count)]
    parts = [value] + [None] * (count - 1)
    for k in range(1, count // 2 + 1):
        parts[count - k] = lax.ppermute(parts[(count - k + 1) % count], COLUMN, up)
        if k < count - k:
            parts[k] = lax.ppermute(parts[k - 1], COLUMN, down)
    return parts


def exchange(value, axes):
    return lax.all_to_all(value, axes, 0, 0, tiled=True)


def local(features, targets, station_ids, lead_heads, station_weight):
    row_count, feat_width = features.shape
    pieces = lax.axis_size(("y", "zl", "c"))
    total_rows = row_count * lax.axis_size(PLANE + COLUMN + ("c",))
    core = lax.axis_index("c").astype(jnp.int32)
    piece_at = lax.axis_index(("y", "zl", "c")).astype(jnp.int32)
    ids = station_ids.reshape(row_count // HALF, HALF)
    target_rows = targets.reshape(row_count // HALF, HALF)
    core_at = core.reshape(1)
    place = jnp.stack([piece_at, core])

    keep, send = gram_of(lead_heads, core_at, station_weight, ids, target_rows, features)
    chip = keep + swap_cores(send)
    partial = whole_call(
        plane_sum_kernel,
        jax.ShapeDtypeStruct((PACKED, HALF), jnp.float32),
        "plane_sum",
        exchange(chip, PLANE),
    )
    own = column_sum(lax.axis_index(COLUMN).astype(jnp.int32).reshape(1), around_column(partial))
    own_inverses = exchange(factor_of(core_at, own, swap_cores(own)), PLANE)
    other_inverses = swap_cores(own_inverses)
    leverage, zscores, inverse_factor = lever_of(
        lead_heads,
        place,
        station_weight,
        ids,
        own_inverses,
        other_inverses,
        features,
        total_rows / (HEADS * feat_width),
        math.sqrt(total_rows / HEADS),
        feat_width // pieces,
    )
    return (leverage.reshape(row_count), zscores, inverse_factor)


def solution(mesh):
    grid = Mesh(mesh.devices.reshape(4, 2, 4, 4, 2), ("x", "zh", "y", "zl", "c"))
    rows = ("x", "zh", "y", "zl", "c")
    return jax.shard_map(
        local,
        mesh=grid,
        in_specs=(P(rows, None), P(rows), P(rows), P(rows), P(("x", "zh"), None)),
        out_specs=(P(rows), P(), P(None, ("y", "zl", "c"), None)),
        check_vma=False,
    )
```

time: 152 us -> 111 us (0.73)
  Pallas kernels: 59.4 us -> 29 us
  blocking collectives: 69.5 us -> 42 us
  starting transfers between devices: 8.8 us -> 22.3 us
  waiting for transfers between devices: 5.22 us -> 15.6 us
  local copies, waits for them, and re-layouts: 3.13 us -> 0.02 us
  other arithmetic: 4.11 us -> 1.44 us
    all_to_all x4 -> x2, blocking collectives: 69.5 us -> 42 us  [exchange(): return lax.all_to_all(value, axes, 0, 0, tiled=True)]
    pallas_call x1, Pallas kernels: 25 us -> 9.08 us  [factor_of(): pl.pallas_call(factor_kernel, out_shape=jax.ShapeDtypeStruct((HEADS, PACK...]
    ppermute x0 -> x7, starting transfers between devices: none -> 11.3 us  [the longest x3 9.54 us: around_column(): parts[k] = lax.ppermute(parts[k - 1], COLUMN, down)]
    ppermute x0 -> x7, waiting for transfers between devices: none -> 9.79 us  [the longest x4 9.78 us: around_column(): parts[count - k] = lax.ppermute(parts[(count - k + 1) % count], COLUMN, up)]
    pallas_call x1, Pallas kernels: 15 us -> 8.61 us  [lever_of(): pl.pallas_call(functools.partial(lever_kernel, lever_scale, factor_scale)...]
    pallas_call x1, Pallas kernels: 16 us -> 11.1 us  [gram_of(): pl.pallas_call(gram_kernel, out_shape=(half, half), grid_spec=pltpu.Prefe...]
    pallas_call x2 -> x1, Pallas kernels: 3.48 us -> 0.06 us  [whole_call(): pl.pallas_call(kernel, out_shape=out_shape, in_specs=[vmem] * len(args),...]
    ppermute x3, starting transfers between devices: 8.8 us -> 11.1 us  [swap_cores(): return lax.ppermute(value, 'c', [(0, 1), (1, 0)])]
  transfers between devices with their start and end apart: 3 -> 10, of which waited for: 3 -> 7; matrix products, arithmetic and copies ran while one was open for 0% -> 0% of each run, Pallas kernels for 0% -> 0%
where the time goes in v2:
time: 111 us
  blocking collectives  42 us (38%)
  Pallas kernels  29 us (26%)
  starting transfers between devices  22.3 us (20%)
  waiting for transfers between devices  15.6 us (14%)
  other arithmetic  1.44 us (1%)
    all_to_all x2, blocking collectives, exchange(): return lax.all_to_all(value, axes, 0, 0, tiled=True)  42 us
    pallas_call x1, Pallas kernels, gram_of(): pl.pallas_call(gram_kernel, out_shape=(half, half), grid_spec=pltpu.Prefe...  11.1 us
    ppermute x3, starting transfers between devices, swap_cores(): return lax.ppermute(value, 'c', [(0, 1), (1, 0)])  11.1 us
    ppermute x4, waiting for transfers between devices, around_column(): parts[count - k] = lax.ppermute(parts[(count - k + 1) % count], COLUMN, up)  9.78 us
    ppermute x3, starting transfers between devices, around_column(): parts[k] = lax.ppermute(parts[k - 1], COLUMN, down)  9.54 us
    pallas_call x1, Pallas kernels, factor_of(): pl.pallas_call(factor_kernel, out_shape=jax.ShapeDtypeStruct((HEADS, PACK...  9.08 us
    pallas_call x1, Pallas kernels, lever_of(): pl.pallas_call(functools.partial(lever_kernel, lever_scale, factor_scale)...  8.61 us
    ppermute x3, waiting for transfers between devices, swap_cores(): return lax.ppermute(value, 'c', [(0, 1), (1, 0)])  5.8 us
  transfers between devices with their start and end apart: 10, of which 7 were waited for; matrix products, arithmetic and copies ran while one was open for 0% of the time, Pallas kernels for 0%

profile of v2, /device:TPU:1, one launch (start us, length us, event | category | flops | bytes accessed | tf_op | source)
XLA Modules:
  0.0 111.1 jit_solution(2923944308528352153)
XLA Ops:
  0.6 11.1 %gram.1 = (f32[16,136,128]{2,1,0:T(8,128)}, f32[16,136,128]{2,1,0:T(8,128)}) custom-call(s32[16384]{0:T(1024)} %head_ref.3, s32[1]{0:T(128)} %bitcast.1.core_ref, f32[1,128]{1,0:T(1,128)} %table_ref.3, s32[128,128]{1,0:T(8,128)} %bitcast.6, bf16[128,128]{1,0:T(8,128)(2,1)} %bitcast.8, bf16[16384,256]{1,0:T(8,128)(2,1)} %feat_ref.3), custom_call_target="tpu_custom_call" | custom-call | flops 2147483648 | bytes 8388608 | tf_op jit(solution)/shard_map/gram/pallas_call | solution.py:103
  11.8 3.2 %collective-permute-start = (f32[16,136,128]{2,1,0:T(8,128)}, f32[16,136,128]{2,1,0:T(8,128)S(1)}, u32[]{:S(2)}, u32[]{:S(2)}) collective-permute-start(f32[16,136,128]{2,1,0:T(8,128)} %get-tuple-element.9), channel_id=1, source_target_pairs={{0,1},{1,0},{2,3},{3,2},{4,5},{5,4},{6,7},{7,6},{8,9},{9,8},{10,11... | collective-permute-start | bytes 3342344 | tf_op jit(solution)/shard_map/ppermute | solution.py:348
  15.0 2.6 %collective-permute-done = f32[16,136,128]{2,1,0:T(8,128)S(1)} collective-permute-done((f32[16,136,128]{2,1,0:T(8,128)}, f32[16,136,128]{2,1,0:T(8,128)S(1)}, u32[]{:S(2)}, u32[]{:S(2)}) %collective-permute-start) | collective-permute-done | bytes 1114144 | tf_op jit(solution)/shard_map/ppermute | solution.py:348
  17.6 1.4 %add.15 = f32[16,136,128]{2,1,0:T(8,128)S(1)} add(f32[16,136,128]{2,1,0:T(8,128)} %get-tuple-element.8, f32[16,136,128]{2,1,0:T(8,128)S(1)} %collective-permute-done) | non-fusion elementwise | flops 278528 | bytes 3342336 | tf_op jit(solution)/shard_map/add | solution.py:379
  19.0 22.0 %all_to_all.10.part_ref = f32[16,136,128]{2,1,0:T(8,128)S(1)} all-to-all(f32[16,136,128]{2,1,0:T(8,128)S(1)} %add.15), channel_id=1, replica_groups=mesh['x'=4,'zh'=2,'y'=4,'zl'=4,'c'=2] {'x','y'}, dimensions={0} | all-to-all | bytes 2228224 | tf_op jit(solution)/shard_map/all_to_all | solution.py:364
  41.0 0.1 plane_sum.1.refs_1_
  41.0 1.7 %collective-permute-start.4 = (f32[136,128]{1,0:T(8,128)S(1)}, f32[136,128]{1,0:T(8,128)S(1)}, u32[]{:S(2)}, u32[]{:S(2)}) collective-permute-start(f32[136,128]{1,0:T(8,128)S(1)} %plane_sum.1.refs_1_), channel_id=1, source_target_pairs={{0,2},{2,4},{4,6},{6,32},{32,34},{34,36},{36,38},{38,0},{1,3},{3,5... | collective-permute-start | bytes 208904 | tf_op jit(solution)/shard_map/ppermute | solution.py:357
  42.7 4.0 %collective-permute-start.1 = (f32[136,128]{1,0:T(8,128)S(1)}, f32[136,128]{1,0:T(8,128)S(1)}, u32[]{:S(2)}, u32[]{:S(2)}) collective-permute-start(f32[136,128]{1,0:T(8,128)S(1)} %plane_sum.1.refs_1_), channel_id=1, source_target_pairs={{0,38},{2,0},{4,2},{6,4},{32,6},{34,32},{36,34},{38,36},{1,39},{3,... | collective-permute-start | bytes 208904 | tf_op jit(solution)/shard_map/ppermute | solution.py:359
  46.8 1.6 %collective-permute-done.4.refs_8_ = f32[136,128]{1,0:T(8,128)S(1)} collective-permute-done((f32[136,128]{1,0:T(8,128)S(1)}, f32[136,128]{1,0:T(8,128)S(1)}, u32[]{:S(2)}, u32[]{:S(2)}) %collective-permute-start.4) | collective-permute-done | bytes 69664 | tf_op jit(solution)/shard_map/ppermute | solution.py:357
  48.4 0.0 collective-permute-start.5
  48.4 0.0 collective-permute-done.1.refs_2_
  48.4 2.8 %collective-permute-start.2 = (f32[136,128]{1,0:T(8,128)S(1)}, f32[136,128]{1,0:T(8,128)S(1)}, u32[]{:S(2)}, u32[]{:S(2)}) collective-permute-start(f32[136,128]{1,0:T(8,128)S(1)} %collective-permute-done.1.refs_2_), channel_id=1, source_target_pairs={{0,38},{2,0},{4,2},{6,4},{32,6},{34,32},{36,34},{38,36},{1,39},{3,... | collective-permute-start | bytes 208904 | tf_op jit(solution)/shard_map/ppermute | solution.py:359
  51.1 1.6 %collective-permute-done.5.refs_7_ = f32[136,128]{1,0:T(8,128)S(1)} collective-permute-done((f32[136,128]{1,0:T(8,128)S(1)}, f32[136,128]{1,0:T(8,128)S(1)}, u32[]{:S(2)}, u32[]{:S(2)}) %collective-permute-start.5) | collective-permute-done | bytes 69664 | tf_op jit(solution)/shard_map/ppermute | solution.py:357
  52.7 0.0 collective-permute-start.6
  52.7 0.0 collective-permute-done.2.refs_3_
  52.7 2.8 %collective-permute-start.3 = (f32[136,128]{1,0:T(8,128)S(1)}, f32[136,128]{1,0:T(8,128)S(1)}, u32[]{:S(2)}, u32[]{:S(2)}) collective-permute-start(f32[136,128]{1,0:T(8,128)S(1)} %collective-permute-done.2.refs_3_), channel_id=1, source_target_pairs={{0,38},{2,0},{4,2},{6,4},{32,6},{34,32},{36,34},{38,36},{1,39},{3,... | collective-permute-start | bytes 208904 | tf_op jit(solution)/shard_map/ppermute | solution.py:359
  55.5 1.6 %collective-permute-done.6.refs_6_ = f32[136,128]{1,0:T(8,128)S(1)} collective-permute-done((f32[136,128]{1,0:T(8,128)S(1)}, f32[136,128]{1,0:T(8,128)S(1)}, u32[]{:S(2)}, u32[]{:S(2)}) %collective-permute-start.6) | collective-permute-done | bytes 69664 | tf_op jit(solution)/shard_map/ppermute | solution.py:357
  57.1 0.0 collective-permute-start.7
  57.1 0.0 collective-permute-done.3.refs_4_
  57.1 4.9 %collective-permute-done.7.refs_5_ = f32[136,128]{1,0:T(8,128)S(1)} collective-permute-done((f32[136,128]{1,0:T(8,128)S(1)}, f32[136,128]{1,0:T(8,128)S(1)}, u32[]{:S(2)}, u32[]{:S(2)}) %collective-permute-start.7) | collective-permute-done | bytes 69664 | tf_op jit(solution)/shard_map/ppermute | solution.py:357
  62.1 0.1 column_sum.1.own_ref
  62.1 6.2 %collective-permute-start.8 = (f32[136,128]{1,0:T(8,128)S(1)}, f32[136,128]{1,0:T(8,128)S(1)}, u32[]{:S(2)}, u32[]{:S(2)}) collective-permute-start(f32[136,128]{1,0:T(8,128)S(1)} %column_sum.1.own_ref), channel_id=1, source_target_pairs={{0,1},{1,0},{2,3},{3,2},{4,5},{5,4},{6,7},{7,6},{8,9},{9,8},{10,11... | collective-permute-start | bytes 208904 | tf_op jit(solution)/shard_map/ppermute | solution.py:348
  68.3 0.9 collective-permute-done.8.other_ref
  69.2 9.1 %factor.1 = f32[16,136,128]{2,1,0:T(8,128)S(1)} custom-call(s32[1]{0:T(128)} %bitcast.1.core_ref, f32[136,128]{1,0:T(8,128)S(1)} %column_sum.1.own_ref, f32[136,128]{1,0:T(8,128)S(1)} %collective-permute-done.8.other_ref), custom_call_target="tpu_custom_call" | custom-call | tf_op jit(solution)/shard_map/factor/pallas_call | solution.py:254
  78.3 0.0 copy-start
  78.3 0.0 copy-start.1
  78.3 0.0 copy-start.2
  78.3 20.1 %all_to_all.11.own_ref = f32[16,136,128]{2,1,0:T(8,128)S(1)} all-to-all(f32[16,136,128]{2,1,0:T(8,128)S(1)} %factor.1), channel_id=1, replica_groups=mesh['x'=4,'zh'=2,'y'=4,'zl'=4,'c'=2] {'x','y'}, dimensions={0} | all-to-all | bytes 2228224 | tf_op jit(solution)/shard_map/all_to_all | solution.py:364
  98.4 1.7 %collective-permute-start.9 = (f32[16,136,128]{2,1,0:T(8,128)S(1)}, f32[16,136,128]{2,1,0:T(8,128)S(1)}, u32[]{:S(2)}, u32[]{:S(2)}) collective-permute-start(f32[16,136,128]{2,1,0:T(8,128)S(1)} %all_to_all.11.own_ref), channel_id=1, source_target_pairs={{0,1},{1,0},{2,3},{3,2},{4,5},{5,4},{6,7},{7,6},{8,9},{9,8},{10,11... | collective-permute-start | bytes 3342344 | tf_op jit(solution)/shard_map/ppermute | solution.py:348
  100.1 0.1 pad_add_fusion.place_ref
  100.1 2.3 %collective-permute-done.9.other_ref = f32[16,136,128]{2,1,0:T(8,128)S(1)} collective-permute-done((f32[16,136,128]{2,1,0:T(8,128)S(1)}, f32[16,136,128]{2,1,0:T(8,128)S(1)}, u32[]{:S(2)}, u32[]{:S(2)}) %collective-permute-start.9) | collective-permute-done | bytes 1114144 | tf_op jit(solution)/shard_map/ppermute | solution.py:348
  102.5 0.0 copy-done
  102.5 0.0 copy-done.1
  102.5 0.0 copy-done.2
  102.5 8.6 %lever.1 = (f32[128,128]{1,0:T(8,128)}, f32[16,256]{1,0:T(8,128)}, f32[16,8,256]{2,1,0:T(8,128)}) custom-call(s32[16384]{0:T(1024)S(1)} %copy-done, s32[2]{0:T(128)S(1)} %pad_add_fusion.place_ref, f32[1,128]{1,0:T(1,128)S(1)} %copy-done.2, s32[128,128]{1,0:T(8,128)S(1)} %bitcast.7, f32[16,136,128]{2,1,0:T(8,128)S(1)} %all_to_all.11.own_ref, ...), custom_call_target="tpu_custom_call" | custom-call | tf_op jit(solution)/shard_map/lever/pallas_call | solution.py:315
Async XLA Ops:
  11.8 5.8 %collective-permute-start = (f32[16,136,128]{2,1,0:T(8,128)}, f32[16,136,128]{2,1,0:T(8,128)S(1)}, u32[]{:S(2)}, u32[]{:S(2)}) collective-permute-start(f32[16,136,128]{2,1,0:T(8,128)} %get-tuple-element.9), channel_id=1, source_target_pairs={{0,1},{1,0},{2,3},{3,2},{4,5},{5,4},{6,7},{7,6},{8,9},{9,8},{10,11... | collective-permute-start | bytes 3342344 | tf_op jit(solution)/shard_map/ppermute | solution.py:348
  41.0 7.4 %collective-permute-start.4 = (f32[136,128]{1,0:T(8,128)S(1)}, f32[136,128]{1,0:T(8,128)S(1)}, u32[]{:S(2)}, u32[]{:S(2)}) collective-permute-start(f32[136,128]{1,0:T(8,128)S(1)} %plane_sum.1.refs_1_), channel_id=1, source_target_pairs={{0,2},{2,4},{4,6},{6,32},{32,34},{34,36},{36,38},{38,0},{1,3},{3,5... | collective-permute-start | bytes 208904 | tf_op jit(solution)/shard_map/ppermute | solution.py:357
  42.7 5.6 %collective-permute-start.1 = (f32[136,128]{1,0:T(8,128)S(1)}, f32[136,128]{1,0:T(8,128)S(1)}, u32[]{:S(2)}, u32[]{:S(2)}) collective-permute-start(f32[136,128]{1,0:T(8,128)S(1)} %plane_sum.1.refs_1_), channel_id=1, source_target_pairs={{0,38},{2,0},{4,2},{6,4},{32,6},{34,32},{36,34},{38,36},{1,39},{3,... | collective-permute-start | bytes 208904 | tf_op jit(solution)/shard_map/ppermute | solution.py:359
  48.4 4.4 %collective-permute-start.5 = (f32[136,128]{1,0:T(8,128)S(1)}, f32[136,128]{1,0:T(8,128)S(1)}, u32[]{:S(2)}, u32[]{:S(2)}) collective-permute-start(f32[136,128]{1,0:T(8,128)S(1)} %collective-permute-done.4.refs_8_), channel_id=1, source_target_pairs={{0,2},{2,4},{4,6},{6,32},{32,34},{34,36},{36,38},{38,0},{1,3},{3,5... | collective-permute-start | bytes 208904 | tf_op jit(solution)/shard_map/ppermute | solution.py:357
  48.4 4.4 %collective-permute-start.2 = (f32[136,128]{1,0:T(8,128)S(1)}, f32[136,128]{1,0:T(8,128)S(1)}, u32[]{:S(2)}, u32[]{:S(2)}) collective-permute-start(f32[136,128]{1,0:T(8,128)S(1)} %collective-permute-done.1.refs_2_), channel_id=1, source_target_pairs={{0,38},{2,0},{4,2},{6,4},{32,6},{34,32},{36,34},{38,36},{1,39},{3,... | collective-permute-start | bytes 208904 | tf_op jit(solution)/shard_map/ppermute | solution.py:359
  52.7 4.4 %collective-permute-start.6 = (f32[136,128]{1,0:T(8,128)S(1)}, f32[136,128]{1,0:T(8,128)S(1)}, u32[]{:S(2)}, u32[]{:S(2)}) collective-permute-start(f32[136,128]{1,0:T(8,128)S(1)} %collective-permute-done.5.refs_7_), channel_id=1, source_target_pairs={{0,2},{2,4},{4,6},{6,32},{32,34},{34,36},{36,38},{38,0},{1,3},{3,5... | collective-permute-start | bytes 208904 | tf_op jit(solution)/shard_map/ppermute | solution.py:357
  52.7 4.4 %collective-permute-start.3 = (f32[136,128]{1,0:T(8,128)S(1)}, f32[136,128]{1,0:T(8,128)S(1)}, u32[]{:S(2)}, u32[]{:S(2)}) collective-permute-start(f32[136,128]{1,0:T(8,128)S(1)} %collective-permute-done.2.refs_3_), channel_id=1, source_target_pairs={{0,38},{2,0},{4,2},{6,4},{32,6},{34,32},{36,34},{38,36},{1,39},{3,... | collective-permute-start | bytes 208904 | tf_op jit(solution)/shard_map/ppermute | solution.py:359
  57.1 5.0 %collective-permute-start.7 = (f32[136,128]{1,0:T(8,128)S(1)}, f32[136,128]{1,0:T(8,128)S(1)}, u32[]{:S(2)}, u32[]{:S(2)}) collective-permute-start(f32[136,128]{1,0:T(8,128)S(1)} %collective-permute-done.6.refs_6_), channel_id=1, source_target_pairs={{0,2},{2,4},{4,6},{6,32},{32,34},{34,36},{36,38},{38,0},{1,3},{3,5... | collective-permute-start | bytes 208904 | tf_op jit(solution)/shard_map/ppermute | solution.py:357
  62.1 7.1 %collective-permute-start.8 = (f32[136,128]{1,0:T(8,128)S(1)}, f32[136,128]{1,0:T(8,128)S(1)}, u32[]{:S(2)}, u32[]{:S(2)}) collective-permute-start(f32[136,128]{1,0:T(8,128)S(1)} %column_sum.1.own_ref), channel_id=1, source_target_pairs={{0,1},{1,0},{2,3},{3,2},{4,5},{5,4},{6,7},{7,6},{8,9},{9,8},{10,11... | collective-permute-start | bytes 208904 | tf_op jit(solution)/shard_map/ppermute | solution.py:348
  78.3 24.1 %copy-start = (s32[16384]{0:T(1024)S(1)}, s32[16384]{0:T(1024)}, u32[]{:S(2)}) copy-start(s32[16384]{0:T(1024)} %head_ref.3) | copy-start | bytes 196612
  78.3 24.1 %copy-start.1 = (s32[16384]{0:T(1024)S(1)}, s32[16384]{0:T(1024)}, u32[]{:S(2)}) copy-start(s32[16384]{0:T(1024)} %param.7) | copy-start | bytes 196612
  78.3 24.1 %copy-start.2 = (f32[1,128]{1,0:T(1,128)S(1)}, f32[1,128]{1,0:T(1,128)}, u32[]{:S(2)}) copy-start(f32[1,128]{1,0:T(1,128)} %table_ref.3) | copy-start | bytes 1540
  98.4 4.0 %collective-permute-start.9 = (f32[16,136,128]{2,1,0:T(8,128)S(1)}, f32[16,136,128]{2,1,0:T(8,128)S(1)}, u32[]{:S(2)}, u32[]{:S(2)}) collective-permute-start(f32[16,136,128]{2,1,0:T(8,128)S(1)} %all_to_all.11.own_ref), channel_id=1, source_target_pairs={{0,1},{1,0},{2,3},{3,2},{4,5},{5,4},{6,7},{7,6},{8,9},{9,8},{10,11... | collective-permute-start | bytes 3342344 | tf_op jit(solution)/shard_map/ppermute | solution.py:348

commit v3 on v2

--- a/solution.py
+++ b/solution.py
@@ -14,8 +14,10 @@
 HALF = 128
 PACKED = HALF + 8
 EXACT = lax.Precision.HIGHEST
+PART = HALF // 2
+PIECE = PART + 8
 PLANE = ("x", "y")
-COLUMN = ("zh", "zl")
+COLUMN = ("zh", "zm", "z0")
 SMALL = 8 << 20
 WIDE = 56 << 20
 LARGE = 51 << 20
@@ -80,26 +82,29 @@
     def _():
         core = core_ref[0]
         row_at, col_at = square_iotas()
-        pair_ref[1, HALF:] = jnp.zeros((8, HALF), jnp.float32)
+        pair_ref[1, :, PART:] = jnp.zeros((2, 8, HALF), jnp.float32)
         for h in range(heads):
             second = total_ref[h, HALF:, HALF:]
             diag = jnp.sum(jnp.where(row_at == col_at, second, 0.0), axis=0, keepdims=True)
             moment = moment_ref[h, 0:1]
-            pair_ref[0, :HALF] = total_ref[h, HALF:, :HALF]
-            pair_ref[0, HALF:] = jnp.concatenate(
+            extra = jnp.concatenate(
                 [diag, moment[:, :HALF], moment[:, HALF:], jnp.zeros((5, HALF), jnp.float32)],
                 axis=0,
             )
-            pair_ref[1, :HALF] = jnp.where(col_at <= row_at, total_ref[h, :HALF, :HALF], second)
-            keep_ref[h] = pair_ref[core]
-            send_ref[h] = pair_ref[1 - core]
+            merged = jnp.where(col_at <= row_at, total_ref[h, :HALF, :HALF], second)
+            for q in range(2):
+                pair_ref[0, q, :PART] = total_ref[h, HALF + q * PART : HALF + (q + 1) * PART, :HALF]
+                pair_ref[0, q, PART:] = extra
+                pair_ref[1, q, :PART] = merged[q * PART : (q + 1) * PART]
+            keep_ref[2 * h : 2 * h + 2] = pair_ref[core]
+            send_ref[2 * h : 2 * h + 2] = pair_ref[1 - core]
 
 
 def gram_of(lead_heads, core, table, ids, targets, features):
     rows, width = features.shape
     blocks = rows // BLK
-    half = jax.ShapeDtypeStruct((HEADS, PACKED, HALF), jnp.float32)
-    half_spec = pl.BlockSpec((HEADS, PACKED, HALF), lambda b, h, c: (0, 0, 0))
+    half = jax.ShapeDtypeStruct((2 * HEADS, PIECE, HALF), jnp.float32)
+    half_spec = pl.BlockSpec((2 * HEADS, PIECE, HALF), lambda b, h, c: (0, 0, 0))
     return pl.pallas_call(
         gram_kernel,
         out_shape=(half, half),
@@ -116,7 +121,7 @@
             scratch_shapes=[
                 pltpu.VMEM((HEADS, width, width), jnp.float32),
                 pltpu.VMEM((HEADS, 8, width), jnp.float32),
-                pltpu.VMEM((2, PACKED, HALF), jnp.float32),
+                pltpu.VMEM((2, 2, PIECE, HALF), jnp.float32),
             ],
         ),
         cost_estimate=pl.CostEstimate(
@@ -131,32 +136,17 @@
     total = part_ref[0]
     for p in range(1, part_ref.shape[0]):
         total = total + part_ref[p]
-    out_ref[...] = total
-
-
-def column_sum_kernel(*refs):
-    place_ref, *part_refs, out_ref, ordered_ref = refs
-    count = len(part_refs)
-    for k in range(count):
-        ordered_ref[lax.rem(place_ref[0] + k, count)] = part_refs[k][...]
-    total = ordered_ref[0]
-    for k in range(1, count):
-        total = total + ordered_ref[k]
-    out_ref[...] = total
-
-
-def column_sum(place, parts):
-    vmem = pl.BlockSpec(memory_space=pltpu.VMEM)
-    shape = parts[0].shape
-    return pl.pallas_call(
-        column_sum_kernel,
-        out_shape=jax.ShapeDtypeStruct(shape, jnp.float32),
-        in_specs=[pl.BlockSpec(memory_space=pltpu.SMEM)] + [vmem] * len(parts),
-        out_specs=vmem,
-        scratch_shapes=[pltpu.VMEM((len(parts),) + shape, jnp.float32)],
-        compiler_params=pltpu.CompilerParams(vmem_limit_bytes=SMALL),
-        name="column_sum",
-    )(place, *parts)
+    for d in range(out_ref.shape[0]):
+        out_ref[d] = total
+
+
+def column_sum_kernel(part_ref, out_ref):
+    total = part_ref[0:2]
+    for p in range(2, part_ref.shape[0], 2):
+        total = total + part_ref[p : p + 2]
+    out_ref[:PART] = total[0, :PART]
+    out_ref[PART:HALF] = total[1, :PART]
+    out_ref[HALF:] = total[0, PART:]
 
 
 def whole_call(kernel, out_shape, name, *args):
@@ -348,28 +338,16 @@
     return lax.ppermute(value, "c", [(0, 1), (1, 0)])
 
 
-def around_column(value):
-    count = lax.axis_size(COLUMN)
-    up = [(i, (i + 1) % count) for i in range(count)]
-    down = [(i, (i - 1) % count) for i in range(count)]
-    parts = [value] + [None] * (count - 1)
-    for k in range(1, count // 2 + 1):
-        parts[count - k] = lax.ppermute(parts[(count - k + 1) % count], COLUMN, up)
-        if k < count - k:
-            parts[k] = lax.ppermute(parts[k - 1], COLUMN, down)
-    return parts
-
-
 def exchange(value, axes):
     return lax.all_to_all(value, axes, 0, 0, tiled=True)
 
 
 def local(features, targets, station_ids, lead_heads, station_weight):
     row_count, feat_width = features.shape
-    pieces = lax.axis_size(("y", "zl", "c"))
+    pieces = lax.axis_size(("y", "zm", "z0", "c"))
     total_rows = row_count * lax.axis_size(PLANE + COLUMN + ("c",))
     core = lax.axis_index("c").astype(jnp.int32)
-    piece_at = lax.axis_index(("y", "zl", "c")).astype(jnp.int32)
+    piece_at = lax.axis_index(("y", "zm", "z0", "c")).astype(jnp.int32)
     ids = station_ids.reshape(row_count // HALF, HALF)
     target_rows = targets.reshape(row_count // HALF, HALF)
     core_at = core.reshape(1)
@@ -377,13 +355,18 @@
 
     keep, send = gram_of(lead_heads, core_at, station_weight, ids, target_rows, features)
     chip = keep + swap_cores(send)
-    partial = whole_call(
+    spread = whole_call(
         plane_sum_kernel,
+        jax.ShapeDtypeStruct((lax.axis_size(COLUMN), PIECE, HALF), jnp.float32),
+        "plane_sum",
+        exchange(chip, PLANE + ("z0",)),
+    )
+    own = whole_call(
+        column_sum_kernel,
         jax.ShapeDtypeStruct((PACKED, HALF), jnp.float32),
-        "plane_sum",
-        exchange(chip, PLANE),
-    )
-    own = column_sum(lax.axis_index(COLUMN).astype(jnp.int32).reshape(1), around_column(partial))
+        "column_sum",
+        exchange(spread, COLUMN),
+    )
     own_inverses = exchange(factor_of(core_at, own, swap_cores(own)), PLANE)
     other_inverses = swap_cores(own_inverses)
     leverage, zscores, inverse_factor = lever_of(
@@ -402,12 +385,12 @@
 
 
 def solution(mesh):
-    grid = Mesh(mesh.devices.reshape(4, 2, 4, 4, 2), ("x", "zh", "y", "zl", "c"))
-    rows = ("x", "zh", "y", "zl", "c")
+    grid = Mesh(mesh.devices.reshape(4, 2, 4, 2, 2, 2), ("x", "zh", "y", "zm", "z0", "c"))
+    rows = ("x", "zh", "y", "zm", "z0", "c")
     return jax.shard_map(
         local,
         mesh=grid,
         in_specs=(P(rows, None), P(rows), P(rows), P(rows), P(("x", "zh"), None)),
-        out_specs=(P(rows), P(), P(None, ("y", "zl", "c"), None)),
+        out_specs=(P(rows), P(), P(None, ("y", "zm", "z0", "c"), None)),
         check_vma=False,
     )

time: 111 us -> 108 us (0.973)
  blocking collectives: 42 us -> 61.8 us
  starting transfers between devices: 22.3 us -> 9.14 us
  waiting for transfers between devices: 15.6 us -> 5.9 us
    all_to_all x2 -> x3, blocking collectives: 42 us -> 61.8 us  [exchange(): return lax.all_to_all(value, axes, 0, 0, tiled=True)]
    ppermute x7 -> x0, starting transfers between devices: 11.3 us -> none  [the longest x3 9.54 us: around_column(): parts[k] = lax.ppermute(parts[k - 1], COLUMN, down)]
    ppermute x7 -> x0, waiting for transfers between devices: 9.79 us -> none  [the longest x4 9.78 us: around_column(): parts[count - k] = lax.ppermute(parts[(count - k + 1) % count], COLUMN, up)]
    ppermute x3, starting transfers between devices: 11.1 us -> 9.14 us  [swap_cores(): return lax.ppermute(value, 'c', [(0, 1), (1, 0)])]
  transfers between devices with their start and end apart: 10 -> 3, of which waited for: 7 -> 3; matrix products, arithmetic and copies ran while one was open for 0% -> 0% of each run, Pallas kernels for 0% -> 0%
where the time goes in v3:
time: 108 us
  blocking collectives  61.8 us (57%)
  Pallas kernels  29 us (27%)
  starting transfers between devices  9.14 us (8%)
  waiting for transfers between devices  5.9 us (5%)
  other arithmetic  1.47 us (1%)
    all_to_all x3, blocking collectives, exchange(): return lax.all_to_all(value, axes, 0, 0, tiled=True)  61.8 us
    pallas_call x1, Pallas kernels, gram_of(): pl.pallas_call(gram_kernel, out_shape=(half, half), grid_spec=pltpu.Prefe...  11.2 us
    ppermute x3, starting transfers between devices, swap_cores(): return lax.ppermute(value, 'c', [(0, 1), (1, 0)])  9.14 us
    pallas_call x1, Pallas kernels, factor_of(): pl.pallas_call(factor_kernel, out_shape=jax.ShapeDtypeStruct((HEADS, PACK...  9.08 us
    pallas_call x1, Pallas kernels, lever_of(): pl.pallas_call(functools.partial(lever_kernel, lever_scale, factor_scale)...  8.61 us
    ppermute x3, waiting for transfers between devices, swap_cores(): return lax.ppermute(value, 'c', [(0, 1), (1, 0)])  5.9 us
  transfers between devices with their start and end apart: 3, of which 3 were waited for; matrix products, arithmetic and copies ran while one was open for 0% of the time, Pallas kernels for 0%

profile of v3, /device:TPU:1, one launch (start us, length us, event | category | flops | bytes accessed | tf_op | source)
XLA Modules:
  0.0 108.0 jit_solution(5752864586017435890)
XLA Ops:
  0.6 11.2 %gram.1 = (f32[32,72,128]{2,1,0:T(8,128)}, f32[32,72,128]{2,1,0:T(8,128)}) custom-call(s32[16384]{0:T(1024)} %head_ref.3, s32[1]{0:T(128)} %bitcast.1.core_ref, f32[1,128]{1,0:T(1,128)} %table_ref.3, s32[128,128]{1,0:T(8,128)} %bitcast.5, bf16[128,128]{1,0:T(8,128)(2,1)} %bitcast.7, bf16[16384,256]{1,0:T(8,128)(2,1)} %feat_ref.3), custom_call_target="tpu_custom_call" | custom-call | flops 2147483648 | bytes 8388608 | tf_op jit(solution)/shard_map/gram/pallas_call | solution.py:108
  11.8 3.2 %collective-permute-start = (f32[32,72,128]{2,1,0:T(8,128)}, f32[32,72,128]{2,1,0:T(8,128)S(1)}, u32[]{:S(2)}, u32[]{:S(2)}) collective-permute-start(f32[32,72,128]{2,1,0:T(8,128)} %get-tuple-element.9), channel_id=1, source_target_pairs={{0,1},{1,0},{2,3},{3,2},{4,5},{5,4},{6,7},{7,6},{8,9},{9,8},{10,11... | collective-permute-start | bytes 3538952 | tf_op jit(solution)/shard_map/ppermute | solution.py:338
  15.1 2.7 %collective-permute-done = f32[32,72,128]{2,1,0:T(8,128)S(1)} collective-permute-done((f32[32,72,128]{2,1,0:T(8,128)}, f32[32,72,128]{2,1,0:T(8,128)S(1)}, u32[]{:S(2)}, u32[]{:S(2)}) %collective-permute-start) | collective-permute-done | bytes 1179680 | tf_op jit(solution)/shard_map/ppermute | solution.py:338
  17.7 1.4 %add.15 = f32[32,72,128]{2,1,0:T(8,128)S(1)} add(f32[32,72,128]{2,1,0:T(8,128)} %get-tuple-element.8, f32[32,72,128]{2,1,0:T(8,128)S(1)} %collective-permute-done) | non-fusion elementwise | flops 294912 | bytes 3538944 | tf_op jit(solution)/shard_map/add | solution.py:357
  19.1 24.9 %all_to_all.15.part_ref = f32[32,72,128]{2,1,0:T(8,128)S(1)} all-to-all(f32[32,72,128]{2,1,0:T(8,128)S(1)} %add.15), channel_id=1, replica_groups=mesh['x'=4,'zh'=2,'y'=4,'zm'=2,'z0'=2,'c'=2] {'x','y','z0'}, dimensions={0} | all-to-all | bytes 2359296 | tf_op jit(solution)/shard_map/all_to_all | solution.py:342
  44.1 0.1 plane_sum.1
  44.1 16.5 %all_to_all.16.part_ref = f32[8,72,128]{2,1,0:T(8,128)S(1)} all-to-all(f32[8,72,128]{2,1,0:T(8,128)S(1)} %plane_sum.1), channel_id=1, replica_groups=mesh['x'=4,'zh'=2,'y'=4,'zm'=2,'z0'=2,'c'=2] {'zh','zm','z0'}, dimensions={0} | all-to-all | bytes 589824 | tf_op jit(solution)/shard_map/all_to_all | solution.py:342
  60.6 4.3 %collective-permute-start.1 = (f32[136,128]{1,0:T(8,128)S(1)}, f32[136,128]{1,0:T(8,128)S(1)}, u32[]{:S(2)}, u32[]{:S(2)}) collective-permute-start(f32[136,128]{1,0:T(8,128)S(1)} %column_sum.1.own_ref), channel_id=1, source_target_pairs={{0,1},{1,0},{2,3},{3,2},{4,5},{5,4},{6,7},{7,6},{8,9},{9,8},{10,11... | collective-permute-start | bytes 208904 | tf_op jit(solution)/shard_map/ppermute | solution.py:338
  64.9 0.9 collective-permute-done.1.other_ref
  65.8 9.1 %factor.1 = f32[16,136,128]{2,1,0:T(8,128)S(1)} custom-call(s32[1]{0:T(128)} %bitcast.1.core_ref, f32[136,128]{1,0:T(8,128)S(1)} %column_sum.1.own_ref, f32[136,128]{1,0:T(8,128)S(1)} %collective-permute-done.1.other_ref), custom_call_target="tpu_custom_call" | custom-call | tf_op jit(solution)/shard_map/factor/pallas_call | solution.py:244
  74.8 0.0 copy-start
  74.9 0.0 copy-start.1
  74.9 0.0 copy-start.2
  74.9 20.4 %all_to_all.17.own_ref = f32[16,136,128]{2,1,0:T(8,128)S(1)} all-to-all(f32[16,136,128]{2,1,0:T(8,128)S(1)} %factor.1), channel_id=1, replica_groups=mesh['x'=4,'zh'=2,'y'=4,'zm'=2,'z0'=2,'c'=2] {'x','y'}, dimensions={0} | all-to-all | bytes 2228224 | tf_op jit(solution)/shard_map/all_to_all | solution.py:342
  95.3 1.7 %collective-permute-start.2 = (f32[16,136,128]{2,1,0:T(8,128)S(1)}, f32[16,136,128]{2,1,0:T(8,128)S(1)}, u32[]{:S(2)}, u32[]{:S(2)}) collective-permute-start(f32[16,136,128]{2,1,0:T(8,128)S(1)} %all_to_all.17.own_ref), channel_id=1, source_target_pairs={{0,1},{1,0},{2,3},{3,2},{4,5},{5,4},{6,7},{7,6},{8,9},{9,8},{10,11... | collective-permute-start | bytes 3342344 | tf_op jit(solution)/shard_map/ppermute | solution.py:338
  97.0 0.1 pad_add_fusion.place_ref
  97.0 2.3 %collective-permute-done.2.other_ref = f32[16,136,128]{2,1,0:T(8,128)S(1)} collective-permute-done((f32[16,136,128]{2,1,0:T(8,128)S(1)}, f32[16,136,128]{2,1,0:T(8,128)S(1)}, u32[]{:S(2)}, u32[]{:S(2)}) %collective-permute-start.2) | collective-permute-done | bytes 1114144 | tf_op jit(solution)/shard_map/ppermute | solution.py:338
  99.3 0.0 copy-done
  99.3 0.0 copy-done.1
  99.3 0.0 copy-done.2
  99.3 8.6 %lever.1 = (f32[128,128]{1,0:T(8,128)}, f32[16,256]{1,0:T(8,128)}, f32[16,8,256]{2,1,0:T(8,128)}) custom-call(s32[16384]{0:T(1024)S(1)} %copy-done, s32[2]{0:T(128)S(1)} %pad_add_fusion.place_ref, f32[1,128]{1,0:T(1,128)S(1)} %copy-done.2, s32[128,128]{1,0:T(8,128)S(1)} %bitcast.6, f32[16,136,128]{2,1,0:T(8,128)S(1)} %all_to_all.17.own_ref, ...), custom_call_target="tpu_custom_call" | custom-call | tf_op jit(solution)/shard_map/lever/pallas_call | solution.py:305
  (1 shorter events, 0.0 us)
Async XLA Ops:
  11.8 5.9 %collective-permute-start = (f32[32,72,128]{2,1,0:T(8,128)}, f32[32,72,128]{2,1,0:T(8,128)S(1)}, u32[]{:S(2)}, u32[]{:S(2)}) collective-permute-start(f32[32,72,128]{2,1,0:T(8,128)} %get-tuple-element.9), channel_id=1, source_target_pairs={{0,1},{1,0},{2,3},{3,2},{4,5},{5,4},{6,7},{7,6},{8,9},{9,8},{10,11... | collective-permute-start | bytes 3538952 | tf_op jit(solution)/shard_map/ppermute | solution.py:338
  60.6 5.2 %collective-permute-start.1 = (f32[136,128]{1,0:T(8,128)S(1)}, f32[136,128]{1,0:T(8,128)S(1)}, u32[]{:S(2)}, u32[]{:S(2)}) collective-permute-start(f32[136,128]{1,0:T(8,128)S(1)} %column_sum.1.own_ref), channel_id=1, source_target_pairs={{0,1},{1,0},{2,3},{3,2},{4,5},{5,4},{6,7},{7,6},{8,9},{9,8},{10,11... | collective-permute-start | bytes 208904 | tf_op jit(solution)/shard_map/ppermute | solution.py:338
  74.8 24.5 %copy-start = (s32[16384]{0:T(1024)S(1)}, s32[16384]{0:T(1024)}, u32[]{:S(2)}) copy-start(s32[16384]{0:T(1024)} %head_ref.3) | copy-start | bytes 196612
  74.9 24.5 %copy-start.1 = (s32[16384]{0:T(1024)S(1)}, s32[16384]{0:T(1024)}, u32[]{:S(2)}) copy-start(s32[16384]{0:T(1024)} %param.7) | copy-start | bytes 196612
  74.9 24.5 %copy-start.2 = (f32[1,128]{1,0:T(1,128)S(1)}, f32[1,128]{1,0:T(1,128)}, u32[]{:S(2)}) copy-start(f32[1,128]{1,0:T(1,128)} %table_ref.3) | copy-start | bytes 1540
  95.3 4.0 %collective-permute-start.2 = (f32[16,136,128]{2,1,0:T(8,128)S(1)}, f32[16,136,128]{2,1,0:T(8,128)S(1)}, u32[]{:S(2)}, u32[]{:S(2)}) collective-permute-start(f32[16,136,128]{2,1,0:T(8,128)S(1)} %all_to_all.17.own_ref), channel_id=1, source_target_pairs={{0,1},{1,0},{2,3},{3,2},{4,5},{5,4},{6,7},{7,6},{8,9},{9,8},{10,11... | collective-permute-start | bytes 3342344 | tf_op jit(solution)/shard_map/ppermute | solution.py:338

commit v4 on v3

--- a/solution.py
+++ b/solution.py
@@ -45,91 +45,100 @@
     return jnp.take_along_axis(jnp.broadcast_to(table, ids.shape), ids, axis=1)
 
 
+def chunk_copy(chunk, rows, source_ref, target_ref, sems):
+    lines = pl.ds(pl.multiple_of(chunk * rows, rows), rows)
+    return pltpu.make_async_copy(source_ref.at[lines], target_ref.at[lines], sems.at[chunk])
+
+
 def gram_kernel(
-    head_ref, core_ref, table_ref, id_ref, target_ref, feat_ref,
-    keep_ref, send_ref, total_ref, moment_ref, pair_ref,
+    core_ref, lead_ref, table_ref, id_ref, target_ref, feats_ref,
+    keep_ref, send_ref, picked_ref,
+    total_ref, moment_ref, pair_ref, feat_ref, head_ref, feat_sems, head_sems,
 ):
-    step = pl.program_id(0)
     heads = total_ref.shape[0]
-
-    @pl.when(step == 0)
-    def _():
-        total_ref[...] = jnp.zeros_like(total_ref)
-        moment_ref[...] = jnp.zeros_like(moment_ref)
-
+    chunk_rows = PER_STEP * BLK
+    chunks = feat_ref.shape[0] // chunk_rows
+    for c in range(chunks):
+        chunk_copy(c, chunk_rows, lead_ref, head_ref, head_sems).start()
+        chunk_copy(c, chunk_rows, feats_ref, feat_ref, feat_sems).start()
+    total_ref[...] = jnp.zeros_like(total_ref)
+    moment_ref[...] = jnp.zeros_like(moment_ref)
     table = table_ref[...]
     sublanes = BLK // HALF
-    for i in range(PER_STEP):
-        lines = slice(i * sublanes, (i + 1) * sublanes)
-        feats = feat_ref[i * BLK : (i + 1) * BLK]
-        weight = row_weights(table, id_ref[lines])
-        target = target_ref[lines].astype(jnp.float32)
-        head = head_ref[(step * PER_STEP + i) * BLK]
-        flipped = feats.T
-        pieces = []
-        for s in range(sublanes):
-            piece = flipped[:, s * HALF : (s + 1) * HALF].astype(jnp.float32)
-            pieces.append((piece * weight[s : s + 1, :]).astype(jnp.bfloat16))
-        weighted = jnp.concatenate(pieces, axis=1)
-        total_ref[head] += jnp.dot(weighted, feats, preferred_element_type=jnp.float32)
-        target_row = jnp.concatenate([target[s : s + 1, :] for s in range(sublanes)], axis=1)
-        target_row = jnp.broadcast_to(target_row, (8, BLK)).astype(jnp.bfloat16)
-        moment_ref[head] += lax.dot_general(
-            target_row, weighted, (((1,), (1,)), ((), ())), preferred_element_type=jnp.float32
+
+    def add_chunk(chunk, carry):
+        chunk_copy(chunk, chunk_rows, lead_ref, head_ref, head_sems).wait()
+        chunk_copy(chunk, chunk_rows, feats_ref, feat_ref, feat_sems).wait()
+        for i in range(PER_STEP):
+            block = chunk * PER_STEP + i
+            lines = pl.ds(pl.multiple_of(block * sublanes, sublanes), sublanes)
+            feats = feat_ref[pl.ds(pl.multiple_of(block * BLK, BLK), BLK)]
+            weight = row_weights(table, id_ref[lines])
+            target = target_ref[lines].astype(jnp.float32)
+            head = head_ref[block * BLK]
+            picked_ref[block] = head
+            flipped = feats.T
+            pieces = []
+            for s in range(sublanes):
+                piece = flipped[:, s * HALF : (s + 1) * HALF].astype(jnp.float32)
+                pieces.append((piece * weight[s : s + 1, :]).astype(jnp.bfloat16))
+            weighted = jnp.concatenate(pieces, axis=1)
+            total_ref[head] += jnp.dot(weighted, feats, preferred_element_type=jnp.float32)
+            target_row = jnp.concatenate([target[s : s + 1, :] for s in range(sublanes)], axis=1)
+            target_row = jnp.broadcast_to(target_row, (8, BLK)).astype(jnp.bfloat16)
+            moment_ref[head] += lax.dot_general(
+                target_row, weighted, (((1,), (1,)), ((), ())), preferred_element_type=jnp.float32
+            )
+        return carry
+
+    lax.fori_loop(0, chunks, add_chunk, 0)
+    core = core_ref[0]
+    row_at, col_at = square_iotas()
+    pair_ref[1, :, PART:] = jnp.zeros((2, 8, HALF), jnp.float32)
+    for h in range(heads):
+        second = total_ref[h, HALF:, HALF:]
+        diag = jnp.sum(jnp.where(row_at == col_at, second, 0.0), axis=0, keepdims=True)
+        moment = moment_ref[h, 0:1]
+        extra = jnp.concatenate(
+            [diag, moment[:, :HALF], moment[:, HALF:], jnp.zeros((5, HALF), jnp.float32)],
+            axis=0,
         )
-
-    @pl.when(step == pl.num_programs(0) - 1)
-    def _():
-        core = core_ref[0]
-        row_at, col_at = square_iotas()
-        pair_ref[1, :, PART:] = jnp.zeros((2, 8, HALF), jnp.float32)
-        for h in range(heads):
-            second = total_ref[h, HALF:, HALF:]
-            diag = jnp.sum(jnp.where(row_at == col_at, second, 0.0), axis=0, keepdims=True)
-            moment = moment_ref[h, 0:1]
-            extra = jnp.concatenate(
-                [diag, moment[:, :HALF], moment[:, HALF:], jnp.zeros((5, HALF), jnp.float32)],
-                axis=0,
-            )
-            merged = jnp.where(col_at <= row_at, total_ref[h, :HALF, :HALF], second)
-            for q in range(2):
-                pair_ref[0, q, :PART] = total_ref[h, HALF + q * PART : HALF + (q + 1) * PART, :HALF]
-                pair_ref[0, q, PART:] = extra
-                pair_ref[1, q, :PART] = merged[q * PART : (q + 1) * PART]
-            keep_ref[2 * h : 2 * h + 2] = pair_ref[core]
-            send_ref[2 * h : 2 * h + 2] = pair_ref[1 - core]
-
-
-def gram_of(lead_heads, core, table, ids, targets, features):
+        merged = jnp.where(col_at <= row_at, total_ref[h, :HALF, :HALF], second)
+        for q in range(2):
+            pair_ref[0, q, :PART] = total_ref[h, HALF + q * PART : HALF + (q + 1) * PART, :HALF]
+            pair_ref[0, q, PART:] = extra
+            pair_ref[1, q, :PART] = merged[q * PART : (q + 1) * PART]
+        keep_ref[2 * h : 2 * h + 2] = pair_ref[core]
+        send_ref[2 * h : 2 * h + 2] = pair_ref[1 - core]
+
+
+def gram_of(core, lead_heads, table, ids, targets, features):
     rows, width = features.shape
-    blocks = rows // BLK
+    chunks = rows // (PER_STEP * BLK)
     half = jax.ShapeDtypeStruct((2 * HEADS, PIECE, HALF), jnp.float32)
-    half_spec = pl.BlockSpec((2 * HEADS, PIECE, HALF), lambda b, h, c: (0, 0, 0))
+    vmem = pl.BlockSpec(memory_space=pltpu.VMEM)
+    smem = pl.BlockSpec(memory_space=pltpu.SMEM)
+    hbm = pl.BlockSpec(memory_space=pl.ANY)
     return pl.pallas_call(
         gram_kernel,
-        out_shape=(half, half),
-        grid_spec=pltpu.PrefetchScalarGridSpec(
-            num_scalar_prefetch=2,
-            grid=(blocks // PER_STEP,),
-            in_specs=[
-                pl.BlockSpec((1, HALF), lambda b, h, c: (0, 0)),
-                pl.BlockSpec((PER_STEP * BLK // HALF, HALF), lambda b, h, c: (b, 0)),
-                pl.BlockSpec((PER_STEP * BLK // HALF, HALF), lambda b, h, c: (b, 0)),
-                pl.BlockSpec((PER_STEP * BLK, width), lambda b, h, c: (b, 0)),
-            ],
-            out_specs=(half_spec, half_spec),
-            scratch_shapes=[
-                pltpu.VMEM((HEADS, width, width), jnp.float32),
-                pltpu.VMEM((HEADS, 8, width), jnp.float32),
-                pltpu.VMEM((2, 2, PIECE, HALF), jnp.float32),
-            ],
-        ),
+        out_shape=(half, half, jax.ShapeDtypeStruct((rows // BLK,), jnp.int32)),
+        in_specs=[smem, hbm, vmem, vmem, vmem, hbm],
+        out_specs=(vmem, vmem, smem),
+        scratch_shapes=[
+            pltpu.VMEM((HEADS, width, width), jnp.float32),
+            pltpu.VMEM((HEADS, 8, width), jnp.float32),
+            pltpu.VMEM((2, 2, PIECE, HALF), jnp.float32),
+            pltpu.VMEM((rows, width), jnp.bfloat16),
+            pltpu.SMEM((rows,), jnp.int32),
+            pltpu.SemaphoreType.DMA((chunks,)),
+            pltpu.SemaphoreType.DMA((chunks,)),
+        ],
+        compiler_params=pltpu.CompilerParams(vmem_limit_bytes=WIDE),
         cost_estimate=pl.CostEstimate(
             flops=2 * rows * width * width, bytes_accessed=2 * rows * width, transcendentals=0
         ),
-        compiler_params=pltpu.CompilerParams(vmem_limit_bytes=WIDE),
         name="gram",
-    )(lead_heads, core, table, ids, targets, features)
+    )(core, lead_heads, table, ids, targets, features)
 
 
 def plane_sum_kernel(part_ref, out_ref):
@@ -252,56 +261,64 @@
 
 
 def lever_kernel(
-    lever_scale, factor_scale, head_ref, place_ref, table_ref, id_ref, own_ref, other_ref, feat_ref,
-    out_ref, score_ref, piece_ref, low_ref, full_ref,
+    lever_scale, factor_scale, picked_ref, place_ref, table_ref, id_ref, own_ref, other_ref, feats_ref,
+    out_ref, score_ref, piece_ref, low_ref, full_ref, feat_ref, feat_sems,
 ):
-    step = pl.program_id(0)
     heads = low_ref.shape[0]
     piece_rows = piece_ref.shape[1]
-
-    @pl.when(step == 0)
-    def _():
-        first_core = place_ref[1] == 0
-        row_at, col_at = square_iotas()
-        own_rows = pl.ds(pl.multiple_of(place_ref[0] * piece_rows, piece_rows), piece_rows)
-        for h in range(heads):
-            own = own_ref[h, :HALF]
-            other = other_ref[h, :HALF]
-            merged = jnp.where(first_core, other, own)
-            second = jnp.where(col_at > row_at, merged, 0.0).T
-            second = jnp.where(col_at == row_at, own_ref[h, HALF : HALF + 1], second)
-            full_ref[h, :HALF, :HALF] = jnp.where(col_at <= row_at, merged, 0.0)
-            full_ref[h, :HALF, HALF:] = jnp.zeros((HALF, HALF), jnp.float32)
-            full_ref[h, HALF:, :HALF] = jnp.where(first_core, own, other)
-            full_ref[h, HALF:, HALF:] = second
-            low_ref[h] = full_ref[h].astype(jnp.bfloat16)
-            score_ref[h : h + 1, :HALF] = own_ref[h, HALF + 1 : HALF + 2]
-            score_ref[h : h + 1, HALF:] = own_ref[h, HALF + 2 : HALF + 3]
-            piece_ref[h] = full_ref[h, own_rows, :] * factor_scale
-
+    chunk_rows = PER_STEP * BLK
+    chunks = feat_ref.shape[0] // chunk_rows
+    for c in range(chunks):
+        chunk_copy(c, chunk_rows, feats_ref, feat_ref, feat_sems).start()
+    first_core = place_ref[1] == 0
+    row_at, col_at = square_iotas()
+    own_rows = pl.ds(pl.multiple_of(place_ref[0] * piece_rows, piece_rows), piece_rows)
+    for h in range(heads):
+        own = own_ref[h, :HALF]
+        other = other_ref[h, :HALF]
+        merged = jnp.where(first_core, other, own)
+        second = jnp.where(col_at > row_at, merged, 0.0).T
+        second = jnp.where(col_at == row_at, own_ref[h, HALF : HALF + 1], second)
+        full_ref[h, :HALF, :HALF] = jnp.where(col_at <= row_at, merged, 0.0)
+        full_ref[h, :HALF, HALF:] = jnp.zeros((HALF, HALF), jnp.float32)
+        full_ref[h, HALF:, :HALF] = jnp.where(first_core, own, other)
+        full_ref[h, HALF:, HALF:] = second
+        low_ref[h] = full_ref[h].astype(jnp.bfloat16)
+        score_ref[h : h + 1, :HALF] = own_ref[h, HALF + 1 : HALF + 2]
+        score_ref[h : h + 1, HALF:] = own_ref[h, HALF + 2 : HALF + 3]
+        piece_ref[h] = full_ref[h, own_rows, :] * factor_scale
     table = table_ref[...]
     sublanes = BLK // HALF
-    for i in range(PER_STEP):
-        lines = slice(i * sublanes, (i + 1) * sublanes)
-        weight = row_weights(table, id_ref[lines])
-        projected = lax.dot_general(
-            low_ref[head_ref[(step * PER_STEP + i) * BLK]],
-            feat_ref[i * BLK : (i + 1) * BLK],
-            (((1,), (1,)), ((), ())),
-            preferred_element_type=jnp.float32,
-        )
-        squares = jnp.sum(projected * projected, axis=0, keepdims=True)
-        squares = jnp.concatenate(
-            [squares[:, s * HALF : (s + 1) * HALF] for s in range(sublanes)], axis=0
-        )
-        out_ref[lines] = weight * squares * lever_scale
+
+    def score_chunk(chunk, carry):
+        chunk_copy(chunk, chunk_rows, feats_ref, feat_ref, feat_sems).wait()
+        for i in range(PER_STEP):
+            block = chunk * PER_STEP + i
+            lines = pl.ds(pl.multiple_of(block * sublanes, sublanes), sublanes)
+            weight = row_weights(table, id_ref[lines])
+            projected = lax.dot_general(
+                low_ref[picked_ref[block]],
+                feat_ref[pl.ds(pl.multiple_of(block * BLK, BLK), BLK)],
+                (((1,), (1,)), ((), ())),
+                preferred_element_type=jnp.float32,
+            )
+            squares = jnp.sum(projected * projected, axis=0, keepdims=True)
+            squares = jnp.concatenate(
+                [squares[:, s * HALF : (s + 1) * HALF] for s in range(sublanes)], axis=0
+            )
+            out_ref[lines] = weight * squares * lever_scale
+        return carry
+
+    lax.fori_loop(0, chunks, score_chunk, 0)
 
 
 def lever_of(
-    lead_heads, place, table, ids, own, other, features, lever_scale, factor_scale, piece_rows
+    picked, place, table, ids, own, other, features, lever_scale, factor_scale, piece_rows
 ):
     rows, width = features.shape
-    blocks = rows // BLK
+    vmem = pl.BlockSpec(memory_space=pltpu.VMEM)
+    smem = pl.BlockSpec(memory_space=pltpu.SMEM)
+    hbm = pl.BlockSpec(memory_space=pl.ANY)
     return pl.pallas_call(
         functools.partial(lever_kernel, lever_scale, factor_scale),
         out_shape=(
@@ -309,29 +326,17 @@
             jax.ShapeDtypeStruct((HEADS, width), jnp.float32),
             jax.ShapeDtypeStruct((HEADS, piece_rows, width), jnp.float32),
         ),
-        grid_spec=pltpu.PrefetchScalarGridSpec(
-            num_scalar_prefetch=2,
-            grid=(blocks // PER_STEP,),
-            in_specs=[
-                pl.BlockSpec((1, HALF), lambda b, h, o: (0, 0)),
-                pl.BlockSpec((PER_STEP * BLK // HALF, HALF), lambda b, h, o: (b, 0)),
-                pl.BlockSpec((HEADS, PACKED, HALF), lambda b, h, o: (0, 0, 0)),
-                pl.BlockSpec((HEADS, PACKED, HALF), lambda b, h, o: (0, 0, 0)),
-                pl.BlockSpec((PER_STEP * BLK, width), lambda b, h, o: (b, 0)),
-            ],
-            out_specs=(
-                pl.BlockSpec((PER_STEP * BLK // HALF, HALF), lambda b, h, o: (b, 0)),
-                pl.BlockSpec((HEADS, width), lambda b, h, o: (0, 0)),
-                pl.BlockSpec((HEADS, piece_rows, width), lambda b, h, o: (0, 0, 0)),
-            ),
-            scratch_shapes=[
-                pltpu.VMEM((HEADS, width, width), jnp.bfloat16),
-                pltpu.VMEM((HEADS, width, width), jnp.float32),
-            ],
-        ),
+        in_specs=[smem, smem, vmem, vmem, vmem, vmem, hbm],
+        out_specs=(vmem, vmem, vmem),
+        scratch_shapes=[
+            pltpu.VMEM((HEADS, width, width), jnp.bfloat16),
+            pltpu.VMEM((HEADS, width, width), jnp.float32),
+            pltpu.VMEM((rows, width), jnp.bfloat16),
+            pltpu.SemaphoreType.DMA((rows // (PER_STEP * BLK),)),
+        ],
         compiler_params=pltpu.CompilerParams(vmem_limit_bytes=LARGE),
         name="lever",
-    )(lead_heads, place, table, ids, own, other, features)
+    )(picked, place, table, ids, own, other, features)
 
 
 def swap_cores(value):
@@ -353,7 +358,7 @@
     core_at = core.reshape(1)
     place = jnp.stack([piece_at, core])
 
-    keep, send = gram_of(lead_heads, core_at, station_weight, ids, target_rows, features)
+    keep, send, picked = gram_of(core_at, lead_heads, station_weight, ids, target_rows, features)
     chip = keep + swap_cores(send)
     spread = whole_call(
         plane_sum_kernel,
@@ -370,7 +375,7 @@
     own_inverses = exchange(factor_of(core_at, own, swap_cores(own)), PLANE)
     other_inverses = swap_cores(own_inverses)
     leverage, zscores, inverse_factor = lever_of(
-        lead_heads,
+        picked,
         place,
         station_weight,
         ids,

time: 108 us -> 104 us (0.963)
  Pallas kernels: 29 us -> 24.6 us
    pallas_call x1, Pallas kernels: 8.61 us -> 5.84 us  [lever_of(): pl.pallas_call(functools.partial(lever_kernel, lever_scale, factor_scale)...]
    pallas_call x1, Pallas kernels: 11.2 us -> 9.61 us  [gram_of(): pl.pallas_call(gram_kernel, out_shape=(half, half, jax.ShapeDtypeStruct((...]
where the time goes in v4:
time: 104 us
  blocking collectives  61.8 us (59%)
  Pallas kernels  24.6 us (24%)
  starting transfers between devices  9.23 us (9%)
  waiting for transfers between devices  5.9 us (6%)
  other arithmetic  1.47 us (1%)
    all_to_all x3, blocking collectives, exchange(): return lax.all_to_all(value, axes, 0, 0, tiled=True)  61.8 us
    pallas_call x1, Pallas kernels, gram_of(): pl.pallas_call(gram_kernel, out_shape=(half, half, jax.ShapeDtypeStruct((...  9.61 us
    ppermute x3, starting transfers between devices, swap_cores(): return lax.ppermute(value, 'c', [(0, 1), (1, 0)])  9.23 us
    pallas_call x1, Pallas kernels, factor_of(): pl.pallas_call(factor_kernel, out_shape=jax.ShapeDtypeStruct((HEADS, PACK...  9.07 us
    ppermute x3, waiting for transfers between devices, swap_cores(): return lax.ppermute(value, 'c', [(0, 1), (1, 0)])  5.9 us
    pallas_call x1, Pallas kernels, lever_of(): pl.pallas_call(functools.partial(lever_kernel, lever_scale, factor_scale)...  5.84 us
  transfers between devices with their start and end apart: 3, of which 3 were waited for; matrix products, arithmetic and copies ran while one was open for 0% of the time, Pallas kernels for 0%

profile of v4, /device:TPU:1, one launch (start us, length us, event | category | flops | bytes accessed | tf_op | source)
XLA Modules:
  0.0 103.7 jit_solution(8800156380987813180)
XLA Ops:
  0.6 9.6 %gram.1 = (f32[32,72,128]{2,1,0:T(8,128)}, f32[32,72,128]{2,1,0:T(8,128)}, s32[16]{0:T(128)}) custom-call(s32[1]{0:T(128)} %bitcast.core_ref, s32[16384]{0:T(1024)} %lead_ref.1, f32[1,128]{1,0:T(1,128)} %table_ref.3, s32[128,128]{1,0:T(8,128)} %bitcast.5, bf16[128,128]{1,0:T(8,128)(2,1)} %bitcast.7, bf16[16384,256]{1,0:T(8,128)(2,1)} %feats_ref.3), custom_call_target="tpu_custom_call" | custom-call | flops 2147483648 | bytes 8388608 | tf_op jit(solution)/shard_map/gram/pallas_call | solution.py:122
  10.3 3.3 %collective-permute-start = (f32[32,72,128]{2,1,0:T(8,128)}, f32[32,72,128]{2,1,0:T(8,128)S(1)}, u32[]{:S(2)}, u32[]{:S(2)}) collective-permute-start(f32[32,72,128]{2,1,0:T(8,128)} %get-tuple-element.11), channel_id=1, source_target_pairs={{0,1},{1,0},{2,3},{3,2},{4,5},{5,4},{6,7},{7,6},{8,9},{9,8},{10,11... | collective-permute-start | bytes 3538952 | tf_op jit(solution)/shard_map/ppermute | solution.py:343
  13.6 2.7 %collective-permute-done = f32[32,72,128]{2,1,0:T(8,128)S(1)} collective-permute-done((f32[32,72,128]{2,1,0:T(8,128)}, f32[32,72,128]{2,1,0:T(8,128)S(1)}, u32[]{:S(2)}, u32[]{:S(2)}) %collective-permute-start) | collective-permute-done | bytes 1179680 | tf_op jit(solution)/shard_map/ppermute | solution.py:343
  16.3 1.4 %add.15 = f32[32,72,128]{2,1,0:T(8,128)S(1)} add(f32[32,72,128]{2,1,0:T(8,128)} %get-tuple-element.10, f32[32,72,128]{2,1,0:T(8,128)S(1)} %collective-permute-done) | non-fusion elementwise | flops 294912 | bytes 3538944 | tf_op jit(solution)/shard_map/add | solution.py:362
  17.7 24.9 %all_to_all.15.part_ref = f32[32,72,128]{2,1,0:T(8,128)S(1)} all-to-all(f32[32,72,128]{2,1,0:T(8,128)S(1)} %add.15), channel_id=1, replica_groups=mesh['x'=4,'zh'=2,'y'=4,'zm'=2,'z0'=2,'c'=2] {'x','y','z0'}, dimensions={0} | all-to-all | bytes 2359296 | tf_op jit(solution)/shard_map/all_to_all | solution.py:347
  42.6 0.1 plane_sum.1
  42.7 16.5 %all_to_all.16.part_ref = f32[8,72,128]{2,1,0:T(8,128)S(1)} all-to-all(f32[8,72,128]{2,1,0:T(8,128)S(1)} %plane_sum.1), channel_id=1, replica_groups=mesh['x'=4,'zh'=2,'y'=4,'zm'=2,'z0'=2,'c'=2] {'zh','zm','z0'}, dimensions={0} | all-to-all | bytes 589824 | tf_op jit(solution)/shard_map/all_to_all | solution.py:347
  59.1 4.3 %collective-permute-start.1 = (f32[136,128]{1,0:T(8,128)S(1)}, f32[136,128]{1,0:T(8,128)S(1)}, u32[]{:S(2)}, u32[]{:S(2)}) collective-permute-start(f32[136,128]{1,0:T(8,128)S(1)} %column_sum.1.own_ref), channel_id=1, source_target_pairs={{0,1},{1,0},{2,3},{3,2},{4,5},{5,4},{6,7},{7,6},{8,9},{9,8},{10,11... | collective-permute-start | bytes 208904 | tf_op jit(solution)/shard_map/ppermute | solution.py:343
  63.4 0.9 collective-permute-done.1.other_ref
  64.3 9.1 %factor.1 = f32[16,136,128]{2,1,0:T(8,128)S(1)} custom-call(s32[1]{0:T(128)} %bitcast.core_ref, f32[136,128]{1,0:T(8,128)S(1)} %column_sum.1.own_ref, f32[136,128]{1,0:T(8,128)S(1)} %collective-permute-done.1.other_ref), custom_call_target="tpu_custom_call" | custom-call | tf_op jit(solution)/shard_map/factor/pallas_call | solution.py:253
  73.4 0.0 copy-start
  73.4 0.0 copy-start.1
  73.4 0.0 copy-start.2
  73.4 20.4 %all_to_all.17.own_ref = f32[16,136,128]{2,1,0:T(8,128)S(1)} all-to-all(f32[16,136,128]{2,1,0:T(8,128)S(1)} %factor.1), channel_id=1, replica_groups=mesh['x'=4,'zh'=2,'y'=4,'zm'=2,'z0'=2,'c'=2] {'x','y'}, dimensions={0} | all-to-all | bytes 2228224 | tf_op jit(solution)/shard_map/all_to_all | solution.py:347
  93.8 1.7 %collective-permute-start.2 = (f32[16,136,128]{2,1,0:T(8,128)S(1)}, f32[16,136,128]{2,1,0:T(8,128)S(1)}, u32[]{:S(2)}, u32[]{:S(2)}) collective-permute-start(f32[16,136,128]{2,1,0:T(8,128)S(1)} %all_to_all.17.own_ref), channel_id=1, source_target_pairs={{0,1},{1,0},{2,3},{3,2},{4,5},{5,4},{6,7},{7,6},{8,9},{9,8},{10,11... | collective-permute-start | bytes 3342344 | tf_op jit(solution)/shard_map/ppermute | solution.py:343
  95.5 0.1 pad_add_fusion.place_ref
  95.5 2.3 %collective-permute-done.2.other_ref = f32[16,136,128]{2,1,0:T(8,128)S(1)} collective-permute-done((f32[16,136,128]{2,1,0:T(8,128)S(1)}, f32[16,136,128]{2,1,0:T(8,128)S(1)}, u32[]{:S(2)}, u32[]{:S(2)}) %collective-permute-start.2) | collective-permute-done | bytes 1114144 | tf_op jit(solution)/shard_map/ppermute | solution.py:343
  97.9 0.0 copy-done
  97.9 0.0 copy-done.1
  97.9 0.0 copy-done.2
  97.9 5.8 %lever.1 = (f32[128,128]{1,0:T(8,128)}, f32[16,256]{1,0:T(8,128)}, f32[16,8,256]{2,1,0:T(8,128)}) custom-call(s32[16]{0:T(128)S(1)} %copy-done.2, s32[2]{0:T(128)S(1)} %pad_add_fusion.place_ref, f32[1,128]{1,0:T(1,128)S(1)} %copy-done.1, s32[128,128]{1,0:T(8,128)S(1)} %bitcast.6, f32[16,136,128]{2,1,0:T(8,128)S(1)} %all_to_all.17.own_ref, ...), custom_call_target="tpu_custom_call" | custom-call | tf_op jit(solution)/shard_map/lever/pallas_call | solution.py:322
  (1 shorter events, 0.0 us)
Async XLA Ops:
  10.3 6.0 %collective-permute-start = (f32[32,72,128]{2,1,0:T(8,128)}, f32[32,72,128]{2,1,0:T(8,128)S(1)}, u32[]{:S(2)}, u32[]{:S(2)}) collective-permute-start(f32[32,72,128]{2,1,0:T(8,128)} %get-tuple-element.11), channel_id=1, source_target_pairs={{0,1},{1,0},{2,3},{3,2},{4,5},{5,4},{6,7},{7,6},{8,9},{9,8},{10,11... | collective-permute-start | bytes 3538952 | tf_op jit(solution)/shard_map/ppermute | solution.py:343
  59.1 5.2 %collective-permute-start.1 = (f32[136,128]{1,0:T(8,128)S(1)}, f32[136,128]{1,0:T(8,128)S(1)}, u32[]{:S(2)}, u32[]{:S(2)}) collective-permute-start(f32[136,128]{1,0:T(8,128)S(1)} %column_sum.1.own_ref), channel_id=1, source_target_pairs={{0,1},{1,0},{2,3},{3,2},{4,5},{5,4},{6,7},{7,6},{8,9},{9,8},{10,11... | collective-permute-start | bytes 208904 | tf_op jit(solution)/shard_map/ppermute | solution.py:343
  73.4 24.5 %copy-start = (s32[16384]{0:T(1024)S(1)}, s32[16384]{0:T(1024)}, u32[]{:S(2)}) copy-start(s32[16384]{0:T(1024)} %param.7) | copy-start | bytes 196612
  73.4 24.5 %copy-start.1 = (f32[1,128]{1,0:T(1,128)S(1)}, f32[1,128]{1,0:T(1,128)}, u32[]{:S(2)}) copy-start(f32[1,128]{1,0:T(1,128)} %table_ref.3) | copy-start | bytes 1540
  73.4 24.5 %copy-start.2 = (s32[16]{0:T(128)S(1)}, s32[16]{0:T(128)}, u32[]{:S(2)}) copy-start(s32[16]{0:T(128)} %get-tuple-element.9.picked_ref) | copy-start | bytes 196
  93.8 4.0 %collective-permute-start.2 = (f32[16,136,128]{2,1,0:T(8,128)S(1)}, f32[16,136,128]{2,1,0:T(8,128)S(1)}, u32[]{:S(2)}, u32[]{:S(2)}) collective-permute-start(f32[16,136,128]{2,1,0:T(8,128)S(1)} %all_to_all.17.own_ref), channel_id=1, source_target_pairs={{0,1},{1,0},{2,3},{3,2},{4,5},{5,4},{6,7},{7,6},{8,9},{9,8},{10,11... | collective-permute-start | bytes 3342344 | tf_op jit(solution)/shard_map/ppermute | solution.py:343

commit v5 on v4

--- a/solution.py
+++ b/solution.py
@@ -18,9 +18,11 @@
 PIECE = PART + 8
 PLANE = ("x", "y")
 COLUMN = ("zh", "zm", "z0")
+PIECES = ("y", "zm", "z0", "c")
 SMALL = 8 << 20
 WIDE = 56 << 20
-LARGE = 51 << 20
+LARGE = 24 << 20
+STAGE = 40 << 20
 
 
 def dot_nn(a, b):
@@ -51,23 +53,24 @@
 
 
 def gram_kernel(
-    core_ref, lead_ref, table_ref, id_ref, target_ref, feats_ref,
+    lead_ref, table_ref, id_ref, target_ref, feats_ref,
     keep_ref, send_ref, picked_ref,
-    total_ref, moment_ref, pair_ref, feat_ref, head_ref, feat_sems, head_sems,
+    total_ref, moment_ref, pair_ref, feat_ref, feat_sems,
 ):
     heads = total_ref.shape[0]
     chunk_rows = PER_STEP * BLK
     chunks = feat_ref.shape[0] // chunk_rows
     for c in range(chunks):
-        chunk_copy(c, chunk_rows, lead_ref, head_ref, head_sems).start()
         chunk_copy(c, chunk_rows, feats_ref, feat_ref, feat_sems).start()
     total_ref[...] = jnp.zeros_like(total_ref)
     moment_ref[...] = jnp.zeros_like(moment_ref)
     table = table_ref[...]
     sublanes = BLK // HALF
+    for block in range(chunks * PER_STEP):
+        leads = lead_ref[block * sublanes : block * sublanes + 1].astype(jnp.float32)
+        picked_ref[block] = jnp.max(leads).astype(jnp.int32)
 
     def add_chunk(chunk, carry):
-        chunk_copy(chunk, chunk_rows, lead_ref, head_ref, head_sems).wait()
         chunk_copy(chunk, chunk_rows, feats_ref, feat_ref, feat_sems).wait()
         for i in range(PER_STEP):
             block = chunk * PER_STEP + i
@@ -75,30 +78,27 @@
             feats = feat_ref[pl.ds(pl.multiple_of(block * BLK, BLK), BLK)]
             weight = row_weights(table, id_ref[lines])
             target = target_ref[lines].astype(jnp.float32)
-            head = head_ref[block * BLK]
-            picked_ref[block] = head
+            head = picked_ref[block]
             flipped = feats.T
             pieces = []
+            pulls = jnp.zeros((flipped.shape[0], HALF), jnp.float32)
             for s in range(sublanes):
                 piece = flipped[:, s * HALF : (s + 1) * HALF].astype(jnp.float32)
                 pieces.append((piece * weight[s : s + 1, :]).astype(jnp.bfloat16))
+                pulls = pulls + pieces[-1].astype(jnp.float32) * target[s : s + 1, :]
             weighted = jnp.concatenate(pieces, axis=1)
             total_ref[head] += jnp.dot(weighted, feats, preferred_element_type=jnp.float32)
-            target_row = jnp.concatenate([target[s : s + 1, :] for s in range(sublanes)], axis=1)
-            target_row = jnp.broadcast_to(target_row, (8, BLK)).astype(jnp.bfloat16)
-            moment_ref[head] += lax.dot_general(
-                target_row, weighted, (((1,), (1,)), ((), ())), preferred_element_type=jnp.float32
-            )
+            moment_ref[head] += pulls
         return carry
 
     lax.fori_loop(0, chunks, add_chunk, 0)
-    core = core_ref[0]
+    core = lax.axis_index("c")
     row_at, col_at = square_iotas()
     pair_ref[1, :, PART:] = jnp.zeros((2, 8, HALF), jnp.float32)
     for h in range(heads):
         second = total_ref[h, HALF:, HALF:]
         diag = jnp.sum(jnp.where(row_at == col_at, second, 0.0), axis=0, keepdims=True)
-        moment = moment_ref[h, 0:1]
+        moment = jnp.sum(moment_ref[h].T, axis=0, keepdims=True)
         extra = jnp.concatenate(
             [diag, moment[:, :HALF], moment[:, HALF:], jnp.zeros((5, HALF), jnp.float32)],
             axis=0,
@@ -112,7 +112,7 @@
         send_ref[2 * h : 2 * h + 2] = pair_ref[1 - core]
 
 
-def gram_of(core, lead_heads, table, ids, targets, features):
+def gram_of(lead_heads, table, ids, targets, features):
     rows, width = features.shape
     chunks = rows // (PER_STEP * BLK)
     half = jax.ShapeDtypeStruct((2 * HEADS, PIECE, HALF), jnp.float32)
@@ -122,15 +122,13 @@
     return pl.pallas_call(
         gram_kernel,
         out_shape=(half, half, jax.ShapeDtypeStruct((rows // BLK,), jnp.int32)),
-        in_specs=[smem, hbm, vmem, vmem, vmem, hbm],
+        in_specs=[vmem, vmem, vmem, vmem, hbm],
         out_specs=(vmem, vmem, smem),
         scratch_shapes=[
             pltpu.VMEM((HEADS, width, width), jnp.float32),
-            pltpu.VMEM((HEADS, 8, width), jnp.float32),
+            pltpu.VMEM((HEADS, width, HALF), jnp.float32),
             pltpu.VMEM((2, 2, PIECE, HALF), jnp.float32),
             pltpu.VMEM((rows, width), jnp.bfloat16),
-            pltpu.SMEM((rows,), jnp.int32),
-            pltpu.SemaphoreType.DMA((chunks,)),
             pltpu.SemaphoreType.DMA((chunks,)),
         ],
         compiler_params=pltpu.CompilerParams(vmem_limit_bytes=WIDE),
@@ -138,7 +136,7 @@
             flops=2 * rows * width * width, bytes_accessed=2 * rows * width, transcendentals=0
         ),
         name="gram",
-    )(core, lead_heads, table, ids, targets, features)
+    )(lead_heads, table, ids, targets, features)
 
 
 def plane_sum_kernel(part_ref, out_ref):
@@ -207,10 +205,12 @@
     return jnp.concatenate(rows, axis=0)
 
 
-def factor_kernel(core_ref, own_ref, other_ref, out_ref):
+def factor_kernel(own_ref, other_ref, feats_ref, out_ref, staged_ref, stage_sem):
+    stage = pltpu.make_async_copy(feats_ref, staged_ref, stage_sem)
+    stage.start()
     row_at, col_at = square_iotas()
     eye = (row_at == col_at).astype(jnp.float32)
-    first_core = core_ref[0] == 0
+    first_core = lax.axis_index("c") == 0
     own = own_ref[:HALF]
     other = other_ref[:HALF]
     cross = jnp.where(first_core, own, other)
@@ -246,33 +246,46 @@
     for p in range(out_ref.shape[0]):
         out_ref[p, :HALF] = main_out
         out_ref[p, HALF:] = extra_out
-
-
-def factor_of(core, own, other):
+    stage.wait()
+
+
+def factor_of(own, other, features):
     vmem = pl.BlockSpec(memory_space=pltpu.VMEM)
     return pl.pallas_call(
         factor_kernel,
-        out_shape=jax.ShapeDtypeStruct((HEADS, PACKED, HALF), jnp.float32),
-        in_specs=[pl.BlockSpec(memory_space=pltpu.SMEM), vmem, vmem],
-        out_specs=vmem,
-        compiler_params=pltpu.CompilerParams(vmem_limit_bytes=SMALL),
+        out_shape=(
+            jax.ShapeDtypeStruct((HEADS, PACKED, HALF), jnp.float32),
+            jax.ShapeDtypeStruct(features.shape, features.dtype),
+        ),
+        in_specs=[
+            vmem,
+            vmem,
+            pl.BlockSpec(memory_space=pl.ANY),
+        ],
+        out_specs=(vmem, vmem),
+        scratch_shapes=[pltpu.SemaphoreType.DMA],
+        compiler_params=pltpu.CompilerParams(vmem_limit_bytes=STAGE),
         name="factor",
-    )(core, own, other)
+    )(own, other, features)
+
+
+def piece_index():
+    at = 0
+    for axis in PIECES:
+        at = at * lax.axis_size(axis) + lax.axis_index(axis)
+    return at
 
 
 def lever_kernel(
-    lever_scale, factor_scale, picked_ref, place_ref, table_ref, id_ref, own_ref, other_ref, feats_ref,
-    out_ref, score_ref, piece_ref, low_ref, full_ref, feat_ref, feat_sems,
+    lever_scale, factor_scale, picked_ref, table_ref, id_ref, own_ref, other_ref, feat_ref,
+    out_ref, score_ref, piece_ref, low_ref, full_ref,
 ):
     heads = low_ref.shape[0]
     piece_rows = piece_ref.shape[1]
-    chunk_rows = PER_STEP * BLK
-    chunks = feat_ref.shape[0] // chunk_rows
-    for c in range(chunks):
-        chunk_copy(c, chunk_rows, feats_ref, feat_ref, feat_sems).start()
-    first_core = place_ref[1] == 0
+    chunks = feat_ref.shape[0] // (PER_STEP * BLK)
+    first_core = lax.axis_index("c") == 0
     row_at, col_at = square_iotas()
-    own_rows = pl.ds(pl.multiple_of(place_ref[0] * piece_rows, piece_rows), piece_rows)
+    own_rows = pl.ds(pl.multiple_of(piece_index() * piece_rows, piece_rows), piece_rows)
     for h in range(heads):
         own = own_ref[h, :HALF]
         other = other_ref[h, :HALF]
@@ -291,7 +304,6 @@
     sublanes = BLK // HALF
 
     def score_chunk(chunk, carry):
-        chunk_copy(chunk, chunk_rows, feats_ref, feat_ref, feat_sems).wait()
         for i in range(PER_STEP):
             block = chunk * PER_STEP + i
             lines = pl.ds(pl.multiple_of(block * sublanes, sublanes), sublanes)
@@ -313,12 +325,11 @@
 
 
 def lever_of(
-    picked, place, table, ids, own, other, features, lever_scale, factor_scale, piece_rows
+    picked, table, ids, own, other, features, lever_scale, factor_scale, piece_rows
 ):
     rows, width = features.shape
     vmem = pl.BlockSpec(memory_space=pltpu.VMEM)
     smem = pl.BlockSpec(memory_space=pltpu.SMEM)
-    hbm = pl.BlockSpec(memory_space=pl.ANY)
     return pl.pallas_call(
         functools.partial(lever_kernel, lever_scale, factor_scale),
         out_shape=(
@@ -326,17 +337,15 @@
             jax.ShapeDtypeStruct((HEADS, width), jnp.float32),
             jax.ShapeDtypeStruct((HEADS, piece_rows, width), jnp.float32),
         ),
-        in_specs=[smem, smem, vmem, vmem, vmem, vmem, hbm],
+        in_specs=[smem, vmem, vmem, vmem, vmem, vmem],
         out_specs=(vmem, vmem, vmem),
         scratch_shapes=[
             pltpu.VMEM((HEADS, width, width), jnp.bfloat16),
             pltpu.VMEM((HEADS, width, width), jnp.float32),
-            pltpu.VMEM((rows, width), jnp.bfloat16),
-            pltpu.SemaphoreType.DMA((rows // (PER_STEP * BLK),)),
         ],
         compiler_params=pltpu.CompilerParams(vmem_limit_bytes=LARGE),
         name="lever",
-    )(picked, place, table, ids, own, other, features)
+    )(picked, table, ids, own, other, features)
 
 
 def swap_cores(value):
@@ -349,18 +358,15 @@
 
 def local(features, targets, station_ids, lead_heads, station_weight):
     row_count, feat_width = features.shape
-    pieces = lax.axis_size(("y", "zm", "z0", "c"))
+    pieces = lax.axis_size(PIECES)
     total_rows = row_count * lax.axis_size(PLANE + COLUMN + ("c",))
-    core = lax.axis_index("c").astype(jnp.int32)
-    piece_at = lax.axis_index(("y", "zm", "z0", "c")).astype(jnp.int32)
     ids = station_ids.reshape(row_count // HALF, HALF)
+    lead_rows = lead_heads.reshape(row_count // HALF, HALF)
     target_rows = targets.reshape(row_count // HALF, HALF)
-    core_at = core.reshape(1)
-    place = jnp.stack([piece_at, core])
-
-    keep, send, picked = gram_of(core_at, lead_heads, station_weight, ids, target_rows, features)
+
+    keep, send, picked = gram_of(lead_rows, station_weight, ids, target_rows, features)
     chip = keep + swap_cores(send)
-    spread = whole_call(
+    partial = whole_call(
         plane_sum_kernel,
         jax.ShapeDtypeStruct((lax.axis_size(COLUMN), PIECE, HALF), jnp.float32),
         "plane_sum",
@@ -370,18 +376,18 @@
         column_sum_kernel,
         jax.ShapeDtypeStruct((PACKED, HALF), jnp.float32),
         "column_sum",
-        exchange(spread, COLUMN),
-    )
-    own_inverses = exchange(factor_of(core_at, own, swap_cores(own)), PLANE)
+        exchange(partial, COLUMN),
+    )
+    spread, staged = factor_of(own, swap_cores(own), features)
+    own_inverses = exchange(spread, PLANE)
     other_inverses = swap_cores(own_inverses)
     leverage, zscores, inverse_factor = lever_of(
         picked,
-        place,
         station_weight,
         ids,
         own_inverses,
         other_inverses,
-        features,
+        staged,
         total_rows / (HEADS * feat_width),
         math.sqrt(total_rows / HEADS),
         feat_width // pieces,
@@ -396,6 +402,6 @@
         local,
         mesh=grid,
         in_specs=(P(rows, None), P(rows), P(rows), P(rows), P(("x", "zh"), None)),
-        out_specs=(P(rows), P(), P(None, ("y", "zm", "z0", "c"), None)),
+        out_specs=(P(rows), P(), P(None, PIECES, None)),
         check_vma=False,
     )

time: 104 us -> 105 us (level)
  Pallas kernels: 24.6 us -> 25.8 us
    pallas_call x1, Pallas kernels: 9.07 us -> 11.8 us  [factor_of(): pl.pallas_call(factor_kernel, out_shape=(jax.ShapeDtypeStruct((HEADS, PAC...]
where the time goes in v5:
time: 105 us
  blocking collectives  61.8 us (59%)
  Pallas kernels  25.8 us (25%)
  starting transfers between devices  9.23 us (9%)
  waiting for transfers between devices  5.97 us (6%)
  other arithmetic  1.39 us (1%)
    all_to_all x3, blocking collectives, exchange(): return lax.all_to_all(value, axes, 0, 0, tiled=True)  61.8 us
    pallas_call x1, Pallas kernels, factor_of(): pl.pallas_call(factor_kernel, out_shape=(jax.ShapeDtypeStruct((HEADS, PAC...  11.8 us
    ppermute x3, starting transfers between devices, swap_cores(): return lax.ppermute(value, 'c', [(0, 1), (1, 0)])  9.23 us
    pallas_call x1, Pallas kernels, gram_of(): pl.pallas_call(gram_kernel, out_shape=(half, half, jax.ShapeDtypeStruct((...  8.95 us
    ppermute x3, waiting for transfers between devices, swap_cores(): return lax.ppermute(value, 'c', [(0, 1), (1, 0)])  5.97 us
    pallas_call x1, Pallas kernels, lever_of(): pl.pallas_call(functools.partial(lever_kernel, lever_scale, factor_scale)...  4.98 us
  transfers between devices with their start and end apart: 3, of which 3 were waited for; matrix products, arithmetic and copies ran while one was open for 0% of the time, Pallas kernels for 0%

profile of v5, /device:TPU:1, one launch (start us, length us, event | category | flops | bytes accessed | tf_op | source)
XLA Modules:
  0.0 104.8 jit_solution(16465559440017381661)
XLA Ops:
  0.6 9.0 %gram.1 = (f32[32,72,128]{2,1,0:T(8,128)}, f32[32,72,128]{2,1,0:T(8,128)}, s32[16]{0:T(128)}) custom-call(s32[128,128]{1,0:T(8,128)} %bitcast.6, f32[1,128]{1,0:T(1,128)} %table_ref.3, s32[128,128]{1,0:T(8,128)} %bitcast.4, bf16[128,128]{1,0:T(8,128)(2,1)} %bitcast.7, bf16[16384,256]{1,0:T(8,128)(2,1)} %feats_ref.3), custom_call_target="tpu_custom_call" | custom-call | flops 2147483648 | bytes 8388608 | tf_op jit(solution)/shard_map/gram/pallas_call | solution.py:122
  9.6 3.3 %collective-permute-start = (f32[32,72,128]{2,1,0:T(8,128)}, f32[32,72,128]{2,1,0:T(8,128)S(1)}, u32[]{:S(2)}, u32[]{:S(2)}) collective-permute-start(f32[32,72,128]{2,1,0:T(8,128)} %get-tuple-element.13), channel_id=1, source_target_pairs={{0,1},{1,0},{2,3},{3,2},{4,5},{5,4},{6,7},{7,6},{8,9},{9,8},{10,11... | collective-permute-start | bytes 3538952 | tf_op jit(solution)/shard_map/ppermute | solution.py:352
  12.9 2.7 %collective-permute-done = f32[32,72,128]{2,1,0:T(8,128)S(1)} collective-permute-done((f32[32,72,128]{2,1,0:T(8,128)}, f32[32,72,128]{2,1,0:T(8,128)S(1)}, u32[]{:S(2)}, u32[]{:S(2)}) %collective-permute-start) | collective-permute-done | bytes 1179680 | tf_op jit(solution)/shard_map/ppermute | solution.py:352
  15.6 1.4 %add.3 = f32[32,72,128]{2,1,0:T(8,128)S(1)} add(f32[32,72,128]{2,1,0:T(8,128)} %get-tuple-element.12, f32[32,72,128]{2,1,0:T(8,128)S(1)} %collective-permute-done) | non-fusion elementwise | flops 294912 | bytes 3538944 | tf_op jit(solution)/shard_map/add | solution.py:368
  17.0 24.9 %all_to_all.15.part_ref = f32[32,72,128]{2,1,0:T(8,128)S(1)} all-to-all(f32[32,72,128]{2,1,0:T(8,128)S(1)} %add.3), channel_id=1, replica_groups=mesh['x'=4,'zh'=2,'y'=4,'zm'=2,'z0'=2,'c'=2] {'x','y','z0'}, dimensions={0} | all-to-all | bytes 2359296 | tf_op jit(solution)/shard_map/all_to_all | solution.py:356
  41.9 0.1 plane_sum.1
  42.0 16.5 %all_to_all.16.part_ref = f32[8,72,128]{2,1,0:T(8,128)S(1)} all-to-all(f32[8,72,128]{2,1,0:T(8,128)S(1)} %plane_sum.1), channel_id=1, replica_groups=mesh['x'=4,'zh'=2,'y'=4,'zm'=2,'z0'=2,'c'=2] {'zh','zm','z0'}, dimensions={0} | all-to-all | bytes 589824 | tf_op jit(solution)/shard_map/all_to_all | solution.py:356
  58.5 4.3 %collective-permute-start.1 = (f32[136,128]{1,0:T(8,128)S(1)}, f32[136,128]{1,0:T(8,128)S(1)}, u32[]{:S(2)}, u32[]{:S(2)}) collective-permute-start(f32[136,128]{1,0:T(8,128)S(1)} %column_sum.1.own_ref), channel_id=1, source_target_pairs={{0,1},{1,0},{2,3},{3,2},{4,5},{5,4},{6,7},{7,6},{8,9},{9,8},{10,11... | collective-permute-start | bytes 208904 | tf_op jit(solution)/shard_map/ppermute | solution.py:352
  62.7 0.9 collective-permute-done.1.other_ref
  63.6 11.8 %factor.1 = (f32[16,136,128]{2,1,0:T(8,128)S(1)}, bf16[16384,256]{1,0:T(8,128)(2,1)S(1)}) custom-call(f32[136,128]{1,0:T(8,128)S(1)} %column_sum.1.own_ref, f32[136,128]{1,0:T(8,128)S(1)} %collective-permute-done.1.other_ref, bf16[16384,256]{1,0:T(8,128)(2,1)} %feats_ref.3), custom_call_target="tpu_custom_call" | custom-call | tf_op jit(solution)/shard_map/factor/pallas_call | solution.py:254
  75.4 0.0 copy-start
  75.4 0.0 copy-start.1
  75.4 0.0 copy-start.2
  75.4 20.4 %all_to_all.17.own_ref = f32[16,136,128]{2,1,0:T(8,128)S(1)} all-to-all(f32[16,136,128]{2,1,0:T(8,128)S(1)} %get-tuple-element.14), channel_id=1, replica_groups=mesh['x'=4,'zh'=2,'y'=4,'zm'=2,'z0'=2,'c'=2] {'x','y'}, dimensions={0} | all-to-all | bytes 2228224 | tf_op jit(solution)/shard_map/all_to_all | solution.py:356
  95.8 1.7 %collective-permute-start.2 = (f32[16,136,128]{2,1,0:T(8,128)S(1)}, f32[16,136,128]{2,1,0:T(8,128)S(1)}, u32[]{:S(2)}, u32[]{:S(2)}) collective-permute-start(f32[16,136,128]{2,1,0:T(8,128)S(1)} %all_to_all.17.own_ref), channel_id=1, source_target_pairs={{0,1},{1,0},{2,3},{3,2},{4,5},{5,4},{6,7},{7,6},{8,9},{9,8},{10,11... | collective-permute-start | bytes 3342344 | tf_op jit(solution)/shard_map/ppermute | solution.py:352
  97.5 2.4 %collective-permute-done.2.other_ref = f32[16,136,128]{2,1,0:T(8,128)S(1)} collective-permute-done((f32[16,136,128]{2,1,0:T(8,128)S(1)}, f32[16,136,128]{2,1,0:T(8,128)S(1)}, u32[]{:S(2)}, u32[]{:S(2)}) %collective-permute-start.2) | collective-permute-done | bytes 1114144 | tf_op jit(solution)/shard_map/ppermute | solution.py:352
  99.9 0.0 copy-done
  99.9 0.0 copy-done.1
  99.9 0.0 copy-done.2
  99.9 5.0 %lever.1 = (f32[128,128]{1,0:T(8,128)}, f32[16,256]{1,0:T(8,128)}, f32[16,8,256]{2,1,0:T(8,128)}) custom-call(s32[16]{0:T(128)S(1)} %copy-done.2, f32[1,128]{1,0:T(1,128)S(1)} %copy-done.1, s32[128,128]{1,0:T(8,128)S(1)} %bitcast.5, f32[16,136,128]{2,1,0:T(8,128)S(1)} %all_to_all.17.own_ref, f32[16,136,128]{2,1,0:T(8,128)S(1)} %collective-permute-done.2.other_ref, ...), custom_call_target="tpu_custom_call" | custom-call | tf_op jit(solution)/shard_map/lever/pallas_call | solution.py:333
  (1 shorter events, 0.0 us)
Async XLA Ops:
  9.6 6.0 %collective-permute-start = (f32[32,72,128]{2,1,0:T(8,128)}, f32[32,72,128]{2,1,0:T(8,128)S(1)}, u32[]{:S(2)}, u32[]{:S(2)}) collective-permute-start(f32[32,72,128]{2,1,0:T(8,128)} %get-tuple-element.13), channel_id=1, source_target_pairs={{0,1},{1,0},{2,3},{3,2},{4,5},{5,4},{6,7},{7,6},{8,9},{9,8},{10,11... | collective-permute-start | bytes 3538952 | tf_op jit(solution)/shard_map/ppermute | solution.py:352
  58.5 5.2 %collective-permute-start.1 = (f32[136,128]{1,0:T(8,128)S(1)}, f32[136,128]{1,0:T(8,128)S(1)}, u32[]{:S(2)}, u32[]{:S(2)}) collective-permute-start(f32[136,128]{1,0:T(8,128)S(1)} %column_sum.1.own_ref), channel_id=1, source_target_pairs={{0,1},{1,0},{2,3},{3,2},{4,5},{5,4},{6,7},{7,6},{8,9},{9,8},{10,11... | collective-permute-start | bytes 208904 | tf_op jit(solution)/shard_map/ppermute | solution.py:352
  75.4 24.5 %copy-start = (s32[16384]{0:T(1024)S(1)}, s32[16384]{0:T(1024)}, u32[]{:S(2)}) copy-start(s32[16384]{0:T(1024)} %param.7) | copy-start | bytes 196612
  75.4 24.5 %copy-start.1 = (f32[1,128]{1,0:T(1,128)S(1)}, f32[1,128]{1,0:T(1,128)}, u32[]{:S(2)}) copy-start(f32[1,128]{1,0:T(1,128)} %table_ref.3) | copy-start | bytes 1540
  75.4 24.5 %copy-start.2 = (s32[16]{0:T(128)S(1)}, s32[16]{0:T(128)}, u32[]{:S(2)}) copy-start(s32[16]{0:T(128)} %get-tuple-element.11.picked_ref) | copy-start | bytes 196
  95.8 4.0 %collective-permute-start.2 = (f32[16,136,128]{2,1,0:T(8,128)S(1)}, f32[16,136,128]{2,1,0:T(8,128)S(1)}, u32[]{:S(2)}, u32[]{:S(2)}) collective-permute-start(f32[16,136,128]{2,1,0:T(8,128)S(1)} %all_to_all.17.own_ref), channel_id=1, source_target_pairs={{0,1},{1,0},{2,3},{3,2},{4,5},{5,4},{6,7},{7,6},{8,9},{9,8},{10,11... | collective-permute-start | bytes 3342344 | tf_op jit(solution)/shard_map/ppermute | solution.py:352

commit v6 on v5

--- a/solution.py
+++ b/solution.py
@@ -20,9 +20,8 @@
 COLUMN = ("zh", "zm", "z0")
 PIECES = ("y", "zm", "z0", "c")
 SMALL = 8 << 20
-WIDE = 56 << 20
+WIDE = 61 << 20
 LARGE = 24 << 20
-STAGE = 40 << 20
 
 
 def dot_nn(a, b):
@@ -205,9 +204,7 @@
     return jnp.concatenate(rows, axis=0)
 
 
-def factor_kernel(own_ref, other_ref, feats_ref, out_ref, staged_ref, stage_sem):
-    stage = pltpu.make_async_copy(feats_ref, staged_ref, stage_sem)
-    stage.start()
+def factor_kernel(own_ref, other_ref, out_ref):
     row_at, col_at = square_iotas()
     eye = (row_at == col_at).astype(jnp.float32)
     first_core = lax.axis_index("c") == 0
@@ -246,27 +243,18 @@
     for p in range(out_ref.shape[0]):
         out_ref[p, :HALF] = main_out
         out_ref[p, HALF:] = extra_out
-    stage.wait()
-
-
-def factor_of(own, other, features):
+
+
+def factor_of(own, other):
     vmem = pl.BlockSpec(memory_space=pltpu.VMEM)
     return pl.pallas_call(
         factor_kernel,
-        out_shape=(
-            jax.ShapeDtypeStruct((HEADS, PACKED, HALF), jnp.float32),
-            jax.ShapeDtypeStruct(features.shape, features.dtype),
-        ),
-        in_specs=[
-            vmem,
-            vmem,
-            pl.BlockSpec(memory_space=pl.ANY),
-        ],
-        out_specs=(vmem, vmem),
-        scratch_shapes=[pltpu.SemaphoreType.DMA],
-        compiler_params=pltpu.CompilerParams(vmem_limit_bytes=STAGE),
+        out_shape=jax.ShapeDtypeStruct((HEADS, PACKED, HALF), jnp.float32),
+        in_specs=[vmem, vmem],
+        out_specs=vmem,
+        compiler_params=pltpu.CompilerParams(vmem_limit_bytes=SMALL),
         name="factor",
-    )(own, other, features)
+    )(own, other)
 
 
 def piece_index():
@@ -378,8 +366,7 @@
         "column_sum",
         exchange(partial, COLUMN),
     )
-    spread, staged = factor_of(own, swap_cores(own), features)
-    own_inverses = exchange(spread, PLANE)
+    own_inverses = exchange(factor_of(own, swap_cores(own)), PLANE)
     other_inverses = swap_cores(own_inverses)
     leverage, zscores, inverse_factor = lever_of(
         picked,
@@ -387,7 +374,7 @@
         ids,
         own_inverses,
         other_inverses,
-        staged,
+        features,
         total_rows / (HEADS * feat_width),
         math.sqrt(total_rows / HEADS),
         feat_width // pieces,

time: 105 us -> 103 us (0.981)
  Pallas kernels: 25.8 us -> 23.1 us
    pallas_call x1, Pallas kernels: 11.8 us -> 9.08 us  [factor_of(): pl.pallas_call(factor_kernel, out_shape=jax.ShapeDtypeStruct((HEADS, PACK...]
where the time goes in v6:
time: 103 us
  blocking collectives  62 us (60%)
  Pallas kernels  23.1 us (22%)
  starting transfers between devices  9.23 us (9%)
  waiting for transfers between devices  5.97 us (6%)
  other arithmetic  1.54 us (1%)
    all_to_all x3, blocking collectives, exchange(): return lax.all_to_all(value, axes, 0, 0, tiled=True)  62 us
    ppermute x3, starting transfers between devices, swap_cores(): return lax.ppermute(value, 'c', [(0, 1), (1, 0)])  9.23 us
    pallas_call x1, Pallas kernels, factor_of(): pl.pallas_call(factor_kernel, out_shape=jax.ShapeDtypeStruct((HEADS, PACK...  9.08 us
    pallas_call x1, Pallas kernels, gram_of(): pl.pallas_call(gram_kernel, out_shape=(half, half, jax.ShapeDtypeStruct((...  8.95 us
    ppermute x3, waiting for transfers between devices, swap_cores(): return lax.ppermute(value, 'c', [(0, 1), (1, 0)])  5.97 us
    pallas_call x1, Pallas kernels, lever_of(): pl.pallas_call(functools.partial(lever_kernel, lever_scale, factor_scale)...  4.98 us
  transfers between devices with their start and end apart: 3, of which 3 were waited for; matrix products, arithmetic and copies ran while one was open for 0% of the time, Pallas kernels for 0%

profile of v6, /device:TPU:1, one launch (start us, length us, event | category | flops | bytes accessed | tf_op | source)
XLA Modules:
  0.0 102.6 jit_solution(3352022161078379633)
XLA Ops:
  0.6 9.0 %gram.1 = (f32[32,72,128]{2,1,0:T(8,128)}, f32[32,72,128]{2,1,0:T(8,128)}, s32[16]{0:T(128)}) custom-call(s32[128,128]{1,0:T(8,128)} %bitcast.6, f32[1,128]{1,0:T(1,128)} %table_ref.3, s32[128,128]{1,0:T(8,128)} %bitcast.4, bf16[128,128]{1,0:T(8,128)(2,1)} %bitcast.7, bf16[16384,256]{1,0:T(8,128)(2,1)} %feat_ref.1), custom_call_target="tpu_custom_call" | custom-call | flops 2147483648 | bytes 8388608 | tf_op jit(solution)/shard_map/gram/pallas_call | solution.py:121
  9.6 3.3 %collective-permute-start = (f32[32,72,128]{2,1,0:T(8,128)}, f32[32,72,128]{2,1,0:T(8,128)S(1)}, u32[]{:S(2)}, u32[]{:S(2)}) collective-permute-start(f32[32,72,128]{2,1,0:T(8,128)} %get-tuple-element.11), channel_id=1, source_target_pairs={{0,1},{1,0},{2,3},{3,2},{4,5},{5,4},{6,7},{7,6},{8,9},{9,8},{10,11... | collective-permute-start | bytes 3538952 | tf_op jit(solution)/shard_map/ppermute | solution.py:340
  12.9 2.7 %collective-permute-done = f32[32,72,128]{2,1,0:T(8,128)S(1)} collective-permute-done((f32[32,72,128]{2,1,0:T(8,128)}, f32[32,72,128]{2,1,0:T(8,128)S(1)}, u32[]{:S(2)}, u32[]{:S(2)}) %collective-permute-start) | collective-permute-done | bytes 1179680 | tf_op jit(solution)/shard_map/ppermute | solution.py:340
  15.6 0.0 copy-start
  15.6 1.5 %add.3 = f32[32,72,128]{2,1,0:T(8,128)S(1)} add(f32[32,72,128]{2,1,0:T(8,128)} %get-tuple-element.10, f32[32,72,128]{2,1,0:T(8,128)S(1)} %collective-permute-done) | non-fusion elementwise | flops 294912 | bytes 3538944 | tf_op jit(solution)/shard_map/add | solution.py:356
  17.1 25.2 %all_to_all.15.part_ref = f32[32,72,128]{2,1,0:T(8,128)S(1)} all-to-all(f32[32,72,128]{2,1,0:T(8,128)S(1)} %add.3), channel_id=1, replica_groups=mesh['x'=4,'zh'=2,'y'=4,'zm'=2,'z0'=2,'c'=2] {'x','y','z0'}, dimensions={0} | all-to-all | bytes 2359296 | tf_op jit(solution)/shard_map/all_to_all | solution.py:344
  42.3 0.1 plane_sum.1
  42.4 16.5 %all_to_all.16.part_ref = f32[8,72,128]{2,1,0:T(8,128)S(1)} all-to-all(f32[8,72,128]{2,1,0:T(8,128)S(1)} %plane_sum.1), channel_id=1, replica_groups=mesh['x'=4,'zh'=2,'y'=4,'zm'=2,'z0'=2,'c'=2] {'zh','zm','z0'}, dimensions={0} | all-to-all | bytes 589824 | tf_op jit(solution)/shard_map/all_to_all | solution.py:344
  58.9 4.3 %collective-permute-start.1 = (f32[136,128]{1,0:T(8,128)S(1)}, f32[136,128]{1,0:T(8,128)S(1)}, u32[]{:S(2)}, u32[]{:S(2)}) collective-permute-start(f32[136,128]{1,0:T(8,128)S(1)} %column_sum.1.own_ref), channel_id=1, source_target_pairs={{0,1},{1,0},{2,3},{3,2},{4,5},{5,4},{6,7},{7,6},{8,9},{9,8},{10,11... | collective-permute-start | bytes 208904 | tf_op jit(solution)/shard_map/ppermute | solution.py:340
  63.1 0.9 collective-permute-done.1.other_ref
  64.0 9.1 %factor.1 = f32[16,136,128]{2,1,0:T(8,128)S(1)} custom-call(f32[136,128]{1,0:T(8,128)S(1)} %column_sum.1.own_ref, f32[136,128]{1,0:T(8,128)S(1)} %collective-permute-done.1.other_ref), custom_call_target="tpu_custom_call" | custom-call | tf_op jit(solution)/shard_map/factor/pallas_call | solution.py:250
  73.1 0.0 copy-start.1
  73.1 0.0 copy-start.2
  73.1 0.0 copy-start.3
  73.2 20.4 %all_to_all.17.own_ref = f32[16,136,128]{2,1,0:T(8,128)S(1)} all-to-all(f32[16,136,128]{2,1,0:T(8,128)S(1)} %factor.1), channel_id=1, replica_groups=mesh['x'=4,'zh'=2,'y'=4,'zm'=2,'z0'=2,'c'=2] {'x','y'}, dimensions={0} | all-to-all | bytes 2228224 | tf_op jit(solution)/shard_map/all_to_all | solution.py:344
  93.6 1.7 %collective-permute-start.2 = (f32[16,136,128]{2,1,0:T(8,128)S(1)}, f32[16,136,128]{2,1,0:T(8,128)S(1)}, u32[]{:S(2)}, u32[]{:S(2)}) collective-permute-start(f32[16,136,128]{2,1,0:T(8,128)S(1)} %all_to_all.17.own_ref), channel_id=1, source_target_pairs={{0,1},{1,0},{2,3},{3,2},{4,5},{5,4},{6,7},{7,6},{8,9},{9,8},{10,11... | collective-permute-start | bytes 3342344 | tf_op jit(solution)/shard_map/ppermute | solution.py:340
  95.2 2.4 %collective-permute-done.2.other_ref = f32[16,136,128]{2,1,0:T(8,128)S(1)} collective-permute-done((f32[16,136,128]{2,1,0:T(8,128)S(1)}, f32[16,136,128]{2,1,0:T(8,128)S(1)}, u32[]{:S(2)}, u32[]{:S(2)}) %collective-permute-start.2) | collective-permute-done | bytes 1114144 | tf_op jit(solution)/shard_map/ppermute | solution.py:340
  97.6 0.0 copy-done
  97.6 0.0 copy-done.1
  97.6 0.0 copy-done.2
  97.6 0.0 copy-done.3
  97.6 5.0 %lever.1 = (f32[128,128]{1,0:T(8,128)}, f32[16,256]{1,0:T(8,128)}, f32[16,8,256]{2,1,0:T(8,128)}) custom-call(s32[16]{0:T(128)S(1)} %copy-done.3, f32[1,128]{1,0:T(1,128)S(1)} %copy-done.2, s32[128,128]{1,0:T(8,128)S(1)} %bitcast.5, f32[16,136,128]{2,1,0:T(8,128)S(1)} %all_to_all.17.own_ref, f32[16,136,128]{2,1,0:T(8,128)S(1)} %collective-permute-done.2.other_ref, ...), custom_call_target="tpu_custom_call" | custom-call | tf_op jit(solution)/shard_map/lever/pallas_call | solution.py:321
  (1 shorter events, 0.0 us)
Async XLA Ops:
  9.6 6.0 %collective-permute-start = (f32[32,72,128]{2,1,0:T(8,128)}, f32[32,72,128]{2,1,0:T(8,128)S(1)}, u32[]{:S(2)}, u32[]{:S(2)}) collective-permute-start(f32[32,72,128]{2,1,0:T(8,128)} %get-tuple-element.11), channel_id=1, source_target_pairs={{0,1},{1,0},{2,3},{3,2},{4,5},{5,4},{6,7},{7,6},{8,9},{9,8},{10,11... | collective-permute-start | bytes 3538952 | tf_op jit(solution)/shard_map/ppermute | solution.py:340
  15.6 82.0 %copy-start = (bf16[16384,256]{1,0:T(8,128)(2,1)S(1)}, bf16[16384,256]{1,0:T(8,128)(2,1)}, u32[]{:S(2)}) copy-start(bf16[16384,256]{1,0:T(8,128)(2,1)} %feat_ref.1) | copy-start | bytes 25165828
  58.9 5.2 %collective-permute-start.1 = (f32[136,128]{1,0:T(8,128)S(1)}, f32[136,128]{1,0:T(8,128)S(1)}, u32[]{:S(2)}, u32[]{:S(2)}) collective-permute-start(f32[136,128]{1,0:T(8,128)S(1)} %column_sum.1.own_ref), channel_id=1, source_target_pairs={{0,1},{1,0},{2,3},{3,2},{4,5},{5,4},{6,7},{7,6},{8,9},{9,8},{10,11... | collective-permute-start | bytes 208904 | tf_op jit(solution)/shard_map/ppermute | solution.py:340
  73.1 24.5 %copy-start.1 = (s32[16384]{0:T(1024)S(1)}, s32[16384]{0:T(1024)}, u32[]{:S(2)}) copy-start(s32[16384]{0:T(1024)} %param.7) | copy-start | bytes 196612
  73.1 24.5 %copy-start.2 = (f32[1,128]{1,0:T(1,128)S(1)}, f32[1,128]{1,0:T(1,128)}, u32[]{:S(2)}) copy-start(f32[1,128]{1,0:T(1,128)} %table_ref.3) | copy-start | bytes 1540
  73.1 24.5 %copy-start.3 = (s32[16]{0:T(128)S(1)}, s32[16]{0:T(128)}, u32[]{:S(2)}) copy-start(s32[16]{0:T(128)} %get-tuple-element.9.picked_ref) | copy-start | bytes 196
  93.6 4.0 %collective-permute-start.2 = (f32[16,136,128]{2,1,0:T(8,128)S(1)}, f32[16,136,128]{2,1,0:T(8,128)S(1)}, u32[]{:S(2)}, u32[]{:S(2)}) collective-permute-start(f32[16,136,128]{2,1,0:T(8,128)S(1)} %all_to_all.17.own_ref), channel_id=1, source_target_pairs={{0,1},{1,0},{2,3},{3,2},{4,5},{5,4},{6,7},{7,6},{8,9},{9,8},{10,11... | collective-permute-start | bytes 3342344 | tf_op jit(solution)/shard_map/ppermute | solution.py:340
